TPU v7x, 32 devices: a whole 2x2x4 slice. The times are simulated.
32 devices in a mesh: row: 4 (over x, core), col: 8 (over z, y).
Axes of the slice: x: 2, y: 2, z: 4, core: 2. Of those that a mesh axis runs over, the one named last changes fastest.
Arguments:
- near: float32 [8, 16, 3, 3, 256, 256], P('row', 'col'), may hold values from -0.01 to 3.7
- interp: float32 [8, 16, 160, 160], P('row', 'col'), may hold values from -0.5 to 0.5
- red_count: int32 [8, 16], P('row', 'col'), may hold values from 96 to 160
- owner_flip: int32 [4, 8, 2], P('row', 'col'), may hold values from 0 to 1, as said below
Outputs:
- parents: float32 [4, 8, 640, 640], P('row', 'col')
Inputs may be any that keep to these rules, and one draw needn't show every extreme that they name: owner_flip[i, j, :] is the same on the four devices of each aligned 2 x 2 group, rows 2 i and 2 i + 1, columns 2 j and 2 j + 1.
All inputs are finite; a program needn't handle non-finite values.
Results may differ from a plain program's by a relative error of at most 0.0001.
Values sent between devices are 32-bit elements; how exact they have to be, the bound alone decides.
A program may use at most 128 MiB of HBM per device.

v0:
```python
import functools

import jax
import jax.numpy as jnp
from jax import lax
from jax.experimental import pallas as pl
from jax.experimental.pallas import tpu as pltpu
from jax.sharding import PartitionSpec as P

FULL = (-1, 1, -1, 1)
EXACT = lax.Precision.HIGHEST
GROUP = 8
BLOCK = 32


def split(value):
    high = value.astype(jnp.bfloat16)
    low = (value - high.astype(jnp.float32)).astype(jnp.bfloat16)
    return high, low


def dot(left, right):
    return jnp.dot(left, right, preferred_element_type=jnp.float32)


def product(left, right):
    left_high, left_low = left
    right_high, right_low = right
    return dot(left_high, right_high) + (dot(left_high, right_low) + dot(left_low, right_high))


def left_stack(panel):
    high, low = split(panel.T)
    return high, low


def panel_at(rect, row, col):
    return (row - rect[0]) * (rect[3] - rect[2] + 1) + col - rect[2]


def apply_source(acc, source, rect, target):
    row, col = target
    row_low, row_high = max(row - 1, rect[0]), min(row + 1, rect[1])
    col_low, col_high = max(col - 1, rect[2]), min(col + 1, rect[3])
    width = col_high - col_low + 1
    left = left_stack(source[panel_at(rect, row, col)])

    def body(i, carry):
        row_two = row_low + i // width
        col_two = col_low + i % width
        right = split(source[panel_at(rect, row_two, col_two)])
        at = (row_two - row + 1) * 3 + col_two - col + 1
        acc[at] = acc[at] - product(left, right)
        return carry

    lax.fori_loop(0, (row_high - row_low + 1) * width, body, 0)


def diagonal_inverse(block):
    size = block.shape[0]
    rows = lax.broadcasted_iota(jnp.int32, (size, size), 0)
    cols = lax.broadcasted_iota(jnp.int32, (size, size), 1)
    eye = (rows == cols).astype(jnp.float32)
    wide = jnp.concatenate([block, eye, jnp.zeros((size, 128 - 2 * size), jnp.float32)], axis=1)
    row_ids = lax.broadcasted_iota(jnp.int32, (size, 128), 0)
    scale = jnp.ones((size, 128), jnp.float32)
    for start in range(0, size, GROUP):
        columns = [
            jnp.broadcast_to(wide[:, start + q : start + q + 1], (size, 128)) for q in range(GROUP)
        ]
        for q in range(GROUP):
            at = start + q
            pivot = columns[q][at : at + 1, :]
            inverse = 1.0 / pivot
            below = jnp.where(row_ids > at, columns[q], 0.0)
            scale = jnp.where(row_ids == at, lax.rsqrt(pivot), scale)
            wide = wide - below * (wide[at : at + 1, :] * inverse)
            for p in range(q + 1, GROUP):
                columns[p] = columns[p] - below * (columns[p][at : at + 1, :] * inverse)
    return (wide * scale)[:, size : 2 * size]


def factor_inverse(matrix):
    size = matrix.shape[0]
    rows = lax.broadcasted_iota(jnp.int32, (size, size), 0)
    cols = lax.broadcasted_iota(jnp.int32, (size, size), 1)
    rest = matrix
    right = (rows == cols).astype(jnp.float32)
    done = []
    for start in range(0, size, BLOCK):
        inverse = diagonal_inverse(rest[:BLOCK, :BLOCK])
        top_right = jnp.dot(inverse, right[:BLOCK], precision=EXACT)
        done.append(top_right)
        if start + BLOCK < size:
            top = jnp.dot(inverse, rest[:BLOCK, BLOCK:], precision=EXACT)
            top_t = top.T
            rest = rest[BLOCK:, BLOCK:] - jnp.dot(top_t, top, precision=EXACT)
            right = right[BLOCK:] - jnp.dot(top_t, top_right, precision=EXACT)
    return jnp.concatenate(done, axis=0)


def load(source, at, buffer, sem):
    view = source if at is None else source.at[at]
    copy = pltpu.make_async_copy(view, buffer, sem)
    copy.start()
    return copy


def eliminate_kernel(home, base_at, sources, rects_out, keep, n_extra, relay, *refs):
    n_src, n_out = len(sources), len(rects_out)
    counts, base, interp_all = refs[:3]
    src = refs[3 : 3 + n_src]
    refs = refs[3 + n_src + n_extra :]
    outs = refs[:n_out]
    kept = refs[n_out] if keep else None
    store, interp, sems = refs[-3:]
    slots = interp.shape[-1]
    points = store.shape[-1]
    low = points - slots
    first = load(base, base_at, store, sems.at[0])
    second = load(interp_all, (home[0], home[1]), interp, sems.at[1])
    if relay is not None:
        outs[1][outs[1].shape[0] - 1] = src[0][relay]
    first.wait()
    second.wait()
    for ref, (rect, target) in zip(src, sources):
        apply_source(store, ref, rect, target)
    if keep:
        for i in range(4):
            a, e = i // 2 - home[0], i % 2 - home[1]
            kept[i] = store[(a + 1) * 3 + e + 1][low:, low:]
    red = counts[home[0], home[1]]
    row_ids = lax.broadcasted_iota(jnp.int32, (slots, slots), 0)
    col_ids = lax.broadcasted_iota(jnp.int32, (slots, slots), 1)
    masked = jnp.where((row_ids < red) & (col_ids + low >= red), interp[...], 0.0)
    centre = store[4]
    reduced = centre[:slots] - jnp.dot(masked, centre[low:], precision=EXACT)
    block = reduced[:, :slots] - lax.dot_general(
        reduced[:, low:], masked, (((1,), (1,)), ((), ())), precision=EXACT
    )
    block = jnp.where(
        (row_ids < red) & (col_ids < red), block, (row_ids == col_ids).astype(jnp.float32)
    )
    block = 0.5 * (block + block.T)
    inverse = split(factor_inverse(block))
    interp_pair = split(masked)
    wide_rows = lax.broadcasted_iota(jnp.int32, (slots, points), 0)
    wide_cols = lax.broadcasted_iota(jnp.int32, (slots, points), 1)
    for k in range(9):
        if k == 4:
            inner = jnp.where((wide_rows < red) & (wide_cols >= red), reduced, 0.0)
        else:
            inner = store[k, :slots] - product(interp_pair, split(store[k, low:]))
            inner = jnp.where(wide_rows < red, inner, 0.0)
        panel = product(inverse, split(inner))
        row, col = k // 3 - 1, k % 3 - 1
        for ref, rect in zip(outs, rects_out):
            if rect[0] <= row <= rect[1] and rect[2] <= col <= rect[3]:
                ref[panel_at(rect, row, col)] = panel


VMEM = pl.BlockSpec(memory_space=pltpu.VMEM)
SMEM = pl.BlockSpec(memory_space=pltpu.SMEM)
ANY = pl.BlockSpec(memory_space=pl.ANY)
PARAMS = pltpu.CompilerParams(vmem_limit_bytes=56 * 2**20)


def cost(products):
    return pl.CostEstimate(
        flops=products * 60 * 10**6, bytes_accessed=10**7, transcendentals=0
    )


def eliminate(home, counts, base, base_at, interp, sources, rects_out, keep, extra=(), relay=None):
    points, slots = base.shape[-1], interp.shape[-1]
    rects_out = [FULL] + list(rects_out)
    out_shape = [
        jax.ShapeDtypeStruct(
            (
                (r[1] - r[0] + 1) * (r[3] - r[2] + 1) + (relay is not None and at == 1),
                slots,
                points,
            ),
            jnp.float32,
        )
        for at, r in enumerate(rects_out)
    ]
    if keep:
        out_shape.append(jax.ShapeDtypeStruct((4, slots, slots), jnp.float32))
    plan = [(rect, target) for _, rect, target in sources]
    return pl.pallas_call(
        functools.partial(eliminate_kernel, home, base_at, plan, rects_out, keep, len(extra), relay),
        out_shape=out_shape,
        in_specs=[SMEM, ANY, ANY] + [VMEM] * len(sources) + [ANY] * len(extra),
        out_specs=[VMEM] * len(out_shape),
        scratch_shapes=[
            pltpu.VMEM((9, points, points), jnp.float32),
            pltpu.VMEM((slots, slots), jnp.float32),
            pltpu.SemaphoreType.DMA((2,)),
        ],
        compiler_params=PARAMS,
        cost_estimate=cost(60),
        name="eliminate_%d%d" % home,
    )(counts, base, interp, *[array for array, _, _ in sources], *extra)


def update_kernel(jobs, n_base, n_src, *refs):
    bases, src = refs[:n_base], refs[n_base : n_base + n_src]
    outs, sems = refs[n_base + n_src : -1], refs[-1]
    copies = [
        load(bases[base], at, out, sems.at[i])
        for i, ((base, at, _), out) in enumerate(zip(jobs, outs))
    ]
    for copy, out, (_, _, work) in zip(copies, outs, jobs):
        copy.wait()
        for which, rect, target in work:
            apply_source(out, src[which], rect, target)


def update(name, bases, sources, jobs):
    points = bases[0].shape[-1]
    return pl.pallas_call(
        functools.partial(update_kernel, jobs, len(bases), len(sources)),
        out_shape=[jax.ShapeDtypeStruct((9, points, points), jnp.float32) for _ in jobs],
        in_specs=[ANY] * len(bases) + [VMEM] * len(sources),
        out_specs=[VMEM] * len(jobs),
        scratch_shapes=[pltpu.SemaphoreType.DMA((len(jobs),))],
        compiler_params=PARAMS,
        cost_estimate=cost(20),
        name=name,
    )(*bases, *sources)


def parent_apply(acc, source, rect, shift, colour):
    boxes = [
        i
        for i in range(4)
        if rect[0] <= i // 2 - shift[0] <= rect[1] and rect[2] <= i % 2 - shift[1] <= rect[3]
    ]
    cols = sorted({i % 2 for i in boxes})
    slots = acc.shape[-1]
    low = source.shape[-1] - slots
    for x in boxes:
        if x > colour:
            continue
        panel = source[panel_at(rect, x // 2 - shift[0], x % 2 - shift[1])]
        left = split(panel.T[low:])

        def body(i, carry, x=x, left=left):
            row = boxes[0] // 2 + i // len(cols)
            col = cols[0] + i % len(cols)
            right = split(source[panel_at(rect, row - shift[0], col - shift[1])][:, low:])
            at = x * 4 + row * 2 + col
            acc[at] = acc[at] - product(left, right)
            return carry

        lax.fori_loop(0, len(boxes), body, 0)


def parent_early_kernel(plan, near, kept_one, kept_two, *refs):
    src, out, buffer, sems = refs[:-3], refs[-3], refs[-2], refs[-1]
    low = buffer.shape[-1] - out.shape[-1]
    copies = [
        load(near, (0, (i // 2 + 1) * 3 + i % 2 + 1), buffer.at[i], sems.at[i]) for i in range(4)
    ]
    for i in range(4):
        copies[i].wait()
        out[i] = buffer[i][low:, low:]
        out[4 + i] = kept_one[i]
        out[8 + i] = kept_two[i]
        out[12 + i] = jnp.zeros(out.shape[1:], jnp.float32)
    for ref, (rect, shift, colour) in zip(src, plan):
        parent_apply(out, ref, rect, shift, colour)


def parent_middle_kernel(plan, early, kept_three, *refs):
    src, out = refs[:-1], refs[-1]
    for i in range(12):
        out[i] = early[i]
    for i in range(4):
        out[12 + i] = kept_three[i]
    for ref, (rect, shift, colour) in zip(src, plan):
        parent_apply(out, ref, rect, shift, colour)


def parent_last_kernel(plan, points, counts, middle, *refs):
    src, out, acc = refs[:-2], refs[-2], refs[-1]
    slots = acc.shape[-1]
    low = points - slots
    for i in range(16):
        acc[i] = middle[i]
    for ref, (rect, shift, colour) in zip(src, plan):
        parent_apply(acc, ref, rect, shift, colour)
    relayed = src[0][3]
    acc[5] = acc[5] - product(split(relayed.T[low:]), split(relayed[:, low:]))
    row_ids = lax.broadcasted_iota(jnp.int32, (slots, slots), 0) + low
    col_ids = lax.broadcasted_iota(jnp.int32, (slots, slots), 1) + low
    for x in range(4):
        for y in range(4):
            keep = (row_ids >= counts[x // 2, x % 2]) & (col_ids >= counts[y // 2, y % 2])
            out[x * slots : (x + 1) * slots, y * slots : (y + 1) * slots] = jnp.where(
                keep, acc[x * 4 + y], 0.0
            )


def send(value, axis, by):
    peers = lax.axis_size(axis)
    pairs = [(i, i + by) for i in range(peers) if 0 <= i + by < peers]
    return lax.ppermute(value, axis, pairs)


def from_partner(value, axis):
    pairs = [(source, source ^ 1) for source in range(lax.axis_size(axis))]
    return lax.ppermute(value, axis, pairs)


def local(near, interp, red_count, owner_flip):
    points, slots = near.shape[-1], interp.shape[-1]
    boxes = near.reshape(4, 9, points, points)

    left0, up0, diag0 = (-1, 1, -1, 0), (-1, 0, -1, 1), (-1, 0, -1, 0)
    right1, up1, diag1 = (0, 1, 0, 1), (-1, 0, -1, 1), (-1, 0, 0, 1)
    left2, down2 = (-1, 1, -1, 0), (1, 1, 0, 1)
    down3, right3 = (1, 1, -1, 1), (-1, 0, 1, 1)
    corner3 = (1, 1, 1, 1)

    w0, l0, u0 = eliminate(
        (0, 0), red_count, boxes, 0, interp, [], [left0, up0], False
    )
    l0 = send(l0, "col", -1)
    u0 = send(u0, "row", -1)
    acc1, acc2, acc3 = update(
        "gap_zero", [boxes], [w0],
        [(0, i, [(0, FULL, (i // 2, i % 2))]) for i in (1, 2, 3)],
    )
    w1, r1, u1, kept1 = eliminate(
        (0, 1), red_count, acc1, None, interp, [(l0, left0, (0, -1))], [right1, up1], True,
        extra=(u0,),
    )
    d0 = send(l0[0:4], "row", -1)
    r1 = send(r1, "col", 1)
    u1 = send(u1, "row", -1)
    d1 = send(u1.reshape(2, 3, slots, points)[:, 1:].reshape(4, slots, points), "col", 1)
    acc2, acc3 = update(
        "gap_one", [acc2, acc3], [u0, w1, l0, u1],
        [
            (0, None, [(0, up0, (-1, 0)), (1, FULL, (1, -1)), (3, up1, (-1, -1))]),
            (1, None, [
                (0, up0, (-1, 1)), (1, FULL, (1, 0)), (2, left0, (1, -1)), (3, up1, (-1, 0)),
            ]),
        ],
    )
    w2, l2, v2, kept2 = eliminate(
        (1, 0), red_count, acc2, None, interp,
        [(r1, right1, (1, 1)), (d1, diag1, (-1, 1))],
        [left2, down2], True, extra=(d0,),
    )
    l2 = send(l2, "col", -1)
    v2 = send(v2, "row", 1)
    (acc3,) = update(
        "gap_two", [acc3], [d0, w2],
        [(0, None, [(0, diag0, (-1, -1)), (1, FULL, (0, 1))])],
    )
    plan_early = [
        (w0, FULL, (0, 0), 0), (w1, FULL, (0, 1), 1), (r1, right1, (0, -1), 1),
        (w2, FULL, (1, 0), 2),
    ]
    early = pl.pallas_call(
        functools.partial(parent_early_kernel, [entry[1:] for entry in plan_early]),
        out_shape=jax.ShapeDtypeStruct((16, slots, slots), jnp.float32),
        in_specs=[ANY] + [VMEM] * (2 + len(plan_early)),
        out_specs=VMEM,
        scratch_shapes=[
            pltpu.VMEM((4, points, points), jnp.float32), pltpu.SemaphoreType.DMA((4,)),
        ],
        compiler_params=PARAMS,
        cost_estimate=cost(30),
        name="parent_early",
    )(boxes, kept1, kept2, *[entry[0] for entry in plan_early])
    w3, v3, r3, kept3 = eliminate(
        (1, 1), red_count, acc3, None, interp, [(l2, left2, (0, -1))],
        [down3, right3], True, extra=(early, v2), relay=4,
    )
    v3 = send(v3, "row", 1)
    r3 = send(r3, "col", 1)
    d3 = send(v3[2:3], "col", 1)

    plan_middle = [
        (v2, down2, (-1, 0), 2), (l2, left2, (1, 2), 2),
        (w3, FULL, (1, 1), 3),
    ]
    middle = pl.pallas_call(
        functools.partial(parent_middle_kernel, [entry[1:] for entry in plan_middle]),
        out_shape=jax.ShapeDtypeStruct((16, slots, slots), jnp.float32),
        in_specs=[VMEM] * (2 + len(plan_middle)),
        out_specs=VMEM,
        compiler_params=PARAMS,
        cost_estimate=cost(30),
        name="parent_middle",
    )(early, kept3, *[entry[0] for entry in plan_middle])
    plan_last = [
        (v3, down3, (-1, 1), 3), (r3, right3, (1, -1), 3), (d3, corner3, (-1, -1), 3),
    ]
    parent = pl.pallas_call(
        functools.partial(parent_last_kernel, [entry[1:] for entry in plan_last], points),
        out_shape=jax.ShapeDtypeStruct((4 * slots, 4 * slots), jnp.float32),
        in_specs=[SMEM] + [VMEM] * (1 + len(plan_last)),
        out_specs=VMEM,
        scratch_shapes=[pltpu.VMEM((16, slots, slots), jnp.float32)],
        compiler_params=PARAMS,
        cost_estimate=cost(10),
        name="parent_last",
    )(red_count, middle, *[entry[0] for entry in plan_last])
    flip = owner_flip[0, 0]
    parent = jnp.where(flip[0] == 1, from_partner(parent, "row"), parent)
    parent = jnp.where(flip[1] == 1, from_partner(parent, "col"), parent)
    return parent[None, None]


def solution(mesh):
    in_specs = (
        P("row", "col", None, None, None, None),
        P("row", "col", None, None),
        P("row", "col"),
        P("row", "col", None),
    )
    out_specs = P("row", "col", None, None)
    return jax.shard_map(local, mesh=mesh, in_specs=in_specs, out_specs=out_specs, check_vma=False)
```

profile of v0, /device:TPU:0, one launch (start us, length us, event | category | flops | bytes accessed | tf_op | source)
XLA Modules:
  0.0 233.0 jit_solution(4056326097515204349)
XLA Ops:
  0.0 12.6 %eliminate_00.1 = (f32[9,160,256]{2,1,0:T(8,128)}, f32[6,160,256]{2,1,0:T(8,128)}, f32[6,160,256]{2,1,0:T(8,128)}) custom-call(s32[2,2]{1,0:T(2,128)} %counts.1, f32[4,9,256,256]{3,2,1,0:T(8,128)} %bitcast.7, f32[2,2,160,160]{3,2,1,0:T(8,128)} %refs_2_.7), custom_call_target="tpu_custom_call" | custom-call | flops 3600000000 | bytes 10000000 | tf_op jit(solution)/shard_map/eliminate_00/pallas_call | solution.py:191
  15.2 10.3 %gap_zero.1 = (f32[9,256,256]{2,1,0:T(8,128)}, f32[9,256,256]{2,1,0:T(8,128)}, f32[9,256,256]{2,1,0:T(8,128)}) custom-call(f32[4,9,256,256]{3,2,1,0:T(8,128)} %bitcast.8, f32[9,160,256]{2,1,0:T(8,128)} %get-tuple-element.25.refs_1_.refs_0_), custom_call_target="tpu_custom_call" | custom-call | flops 1200000000 | bytes 10000000 | tf_op jit(solution)/shard_map/gap_zero/pallas_call | solution.py:222
  25.5 13.9 %collective-permute-done.refs_3_.refs_4_ = f32[6,160,256]{2,1,0:T(8,128)S(1)} collective-permute-done((f32[6,160,256]{2,1,0:T(8,128)}, f32[6,160,256]{2,1,0:T(8,128)S(1)}, u32[]{:S(2)}, u32[]{:S(2)}) %collective-permute-start) | collective-permute-done | bytes 983072 | tf_op jit(solution)/shard_map/ppermute | solution.py:309
  40.8 15.0 %eliminate_01.1 = (f32[9,160,256]{2,1,0:T(8,128)}, f32[4,160,256]{2,1,0:T(8,128)}, f32[6,160,256]{2,1,0:T(8,128)}, f32[4,160,160]{2,1,0:T(8,128)}) custom-call(s32[2,2]{1,0:T(2,128)} %counts.1, f32[9,256,256]{2,1,0:T(8,128)} %get-tuple-element.26.refs_1_, f32[2,2,160,160]{3,2,1,0:T(8,128)} %refs_2_.7, f32[6,160,256]{2,1,0:T(8,128)} %copy-done, ...), custom_call_target="tpu_custom_call" | custom-call | flops 3600000000 | bytes 10000000 | tf_op jit(solution)/shard_map/eliminate_01/pallas_call | solution.py:191
  57.0 4.6 %collective-permute-start.3 = (f32[4,160,256]{2,1,0:T(8,128)}, f32[4,160,256]{2,1,0:T(8,128)S(1)}, u32[]{:S(2)}, u32[]{:S(2)}) collective-permute-start(f32[4,160,256]{2,1,0:T(8,128)} %get-tuple-element.35), channel_id=1, source_target_pairs={{0,1},{1,2},{2,3},{3,4},{4,5},{5,6},{6,7},{8,9},{9,10},{10,11},{11... | collective-permute-start | bytes 1966088 | tf_op jit(solution)/shard_map/ppermute | solution.py:309
  64.2 2.7 %collective-permute-start.4 = (f32[4,160,256]{2,1,0:T(8,128)S(1)}, f32[4,160,256]{2,1,0:T(8,128)S(1)}, u32[]{:S(2)}, u32[]{:S(2)}) collective-permute-start(f32[4,160,256]{2,1,0:T(8,128)S(1)} %bitcast.11), channel_id=1, source_target_pairs={{0,1},{1,2},{2,3},{3,4},{4,5},{5,6},{6,7},{8,9},{9,10},{10,11},{11... | collective-permute-start | bytes 1966088 | tf_op jit(solution)/shard_map/ppermute | solution.py:309
  66.9 15.8 %gap_one.1 = (f32[9,256,256]{2,1,0:T(8,128)}, f32[9,256,256]{2,1,0:T(8,128)}) custom-call(f32[9,256,256]{2,1,0:T(8,128)} %get-tuple-element.30.refs_0_, f32[9,256,256]{2,1,0:T(8,128)} %get-tuple-element.31.refs_1_, f32[6,160,256]{2,1,0:T(8,128)} %copy-done.4, f32[9,160,256]{2,1,0:T(8,128)} %get-tuple-element.32.refs_3_.refs_1_, f32[6,160,256]{2,1,0:T(8,128)} %copy-done, ...), custom_call_target="tpu_custom_call" | custom-call | flops 1200000000 | bytes 10000000 | tf_op jit(solution)/shard_map/gap_one/pallas_call | solution.py:222
  82.7 8.1 %collective-permute-done.4.refs_4_ = f32[4,160,256]{2,1,0:T(8,128)S(1)} collective-permute-done((f32[4,160,256]{2,1,0:T(8,128)S(1)}, f32[4,160,256]{2,1,0:T(8,128)S(1)}, u32[]{:S(2)}, u32[]{:S(2)}) %collective-permute-start.4) | collective-permute-done | bytes 655392 | tf_op jit(solution)/shard_map/ppermute | solution.py:309
  91.6 15.6 %eliminate_10.1 = (f32[9,160,256]{2,1,0:T(8,128)}, f32[6,160,256]{2,1,0:T(8,128)}, f32[2,160,256]{2,1,0:T(8,128)}, f32[4,160,160]{2,1,0:T(8,128)}) custom-call(s32[2,2]{1,0:T(2,128)} %counts.1, f32[9,256,256]{2,1,0:T(8,128)} %get-tuple-element.34.refs_1_, f32[2,2,160,160]{3,2,1,0:T(8,128)} %refs_2_.7, f32[4,160,256]{2,1,0:T(8,128)} %copy-done.5, ...), custom_call_target="tpu_custom_call" | custom-call | flops 3600000000 | bytes 10000000 | tf_op jit(solution)/shard_map/eliminate_10/pallas_call | solution.py:191
  108.6 3.6 %collective-permute-start.7 = (f32[2,160,256]{2,1,0:T(8,128)}, f32[2,160,256]{2,1,0:T(8,128)S(1)}, u32[]{:S(2)}, u32[]{:S(2)}) collective-permute-start(f32[2,160,256]{2,1,0:T(8,128)} %get-tuple-element.40), channel_id=1, source_target_pairs={{0,8},{8,16},{16,24},{1,9},{9,17},{17,25},{2,10},{10,18},{18,26},{... | collective-permute-start | bytes 983048 | tf_op jit(solution)/shard_map/ppermute | solution.py:309
  112.2 7.6 %gap_two.1.refs_1_ = f32[9,256,256]{2,1,0:T(8,128)} custom-call(f32[9,256,256]{2,1,0:T(8,128)} %get-tuple-element.38.refs_0_, f32[4,160,256]{2,1,0:T(8,128)} %copy-done.6, f32[9,160,256]{2,1,0:T(8,128)} %get-tuple-element.37.refs_3_.refs_2_), custom_call_target="tpu_custom_call" | custom-call | flops 1200000000 | bytes 10000000 | tf_op jit(solution)/shard_map/gap_two/pallas_call | solution.py:222
  119.8 14.9 %parent_early.1.refs_4_.early = f32[16,160,160]{2,1,0:T(8,128)} custom-call(f32[4,9,256,256]{3,2,1,0:T(8,128)} %bitcast.9, f32[4,160,160]{2,1,0:T(8,128)} %get-tuple-element.29.kept_one, f32[4,160,160]{2,1,0:T(8,128)} %get-tuple-element.36.kept_two, f32[9,160,256]{2,1,0:T(8,128)} %get-tuple-element.25.refs_1_.refs_0_, ...), custom_call_target="tpu_custom_call" | custom-call | flops 1800000000 | bytes 10000000 | tf_op jit(solution)/shard_map/parent_early/pallas_call | solution.py:368
  136.4 14.8 %eliminate_11.1 = (f32[9,160,256]{2,1,0:T(8,128)}, f32[4,160,256]{2,1,0:T(8,128)}, f32[2,160,256]{2,1,0:T(8,128)}, f32[4,160,160]{2,1,0:T(8,128)}) custom-call(s32[2,2]{1,0:T(2,128)} %counts.1, f32[9,256,256]{2,1,0:T(8,128)} %gap_two.1.refs_1_, f32[2,2,160,160]{3,2,1,0:T(8,128)} %refs_2_.7, f32[6,160,256]{2,1,0:T(8,128)} %copy-done.3, ...), custom_call_target="tpu_custom_call" | custom-call | flops 3600000000 | bytes 10000000 | tf_op jit(solution)/shard_map/eliminate_11/pallas_call | solution.py:191
  151.2 2.4 %collective-permute-start.8 = (f32[4,160,256]{2,1,0:T(8,128)}, f32[4,160,256]{2,1,0:T(8,128)S(1)}, u32[]{:S(2)}, u32[]{:S(2)}) collective-permute-start(f32[4,160,256]{2,1,0:T(8,128)} %get-tuple-element.43), channel_id=1, source_target_pairs={{0,8},{8,16},{16,24},{1,9},{9,17},{17,25},{2,10},{10,18},{18,26},{... | collective-permute-start | bytes 1966088 | tf_op jit(solution)/shard_map/ppermute | solution.py:309
  153.6 5.0 %collective-permute-start.9 = (f32[2,160,256]{2,1,0:T(8,128)}, f32[2,160,256]{2,1,0:T(8,128)S(1)}, u32[]{:S(2)}, u32[]{:S(2)}) collective-permute-start(f32[2,160,256]{2,1,0:T(8,128)} %get-tuple-element.44), channel_id=1, source_target_pairs={{0,1},{1,2},{2,3},{3,4},{4,5},{5,6},{6,7},{8,9},{9,10},{10,11},{11... | collective-permute-start | bytes 983048 | tf_op jit(solution)/shard_map/ppermute | solution.py:309
  158.7 5.1 %collective-permute-start.10 = (f32[1,160,256]{2,1,0:T(8,128)S(1)}, f32[1,160,256]{2,1,0:T(8,128)S(1)}, u32[]{:S(2)}, u32[]{:S(2)}) collective-permute-start(f32[1,160,256]{2,1,0:T(8,128)S(1)} %slice.24), channel_id=1, source_target_pairs={{0,1},{1,2},{2,3},{3,4},{4,5},{5,6},{6,7},{8,9},{9,10},{10,11},{11... | collective-permute-start | bytes 491528 | tf_op jit(solution)/shard_map/ppermute | solution.py:309
  163.8 12.3 %parent_middle.1.middle = f32[16,160,160]{2,1,0:T(8,128)} custom-call(f32[16,160,160]{2,1,0:T(8,128)} %parent_early.1.refs_4_.early, f32[4,160,160]{2,1,0:T(8,128)} %get-tuple-element.41.kept_three, f32[2,160,256]{2,1,0:T(8,128)} %copy-done.7, f32[6,160,256]{2,1,0:T(8,128)} %copy-done.3, f32[9,160,256]{2,1,0:T(8,128)} %get-tuple-element.42.refs_2_), custom_call_target="tpu_custom_call" | custom-call | flops 1800000000 | bytes 10000000 | tf_op jit(solution)/shard_map/parent_middle/pallas_call | solution.py:392
  177.4 7.2 %parent_last.1 = f32[640,640]{1,0:T(8,128)} custom-call(s32[2,2]{1,0:T(2,128)} %counts.1, f32[16,160,160]{2,1,0:T(8,128)} %parent_middle.1.middle, f32[4,160,256]{2,1,0:T(8,128)} %copy-done.2, f32[2,160,256]{2,1,0:T(8,128)} %copy-done.8, f32[1,160,256]{2,1,0:T(8,128)} %copy-done.9), custom_call_target="tpu_custom_call" | custom-call | flops 600000000 | bytes 10000000 | tf_op jit(solution)/shard_map/parent_last/pallas_call | solution.py:404
  184.7 2.7 %collective-permute-start.11 = (f32[640,640]{1,0:T(8,128)}, f32[640,640]{1,0:T(8,128)S(1)}, u32[]{:S(2)}, u32[]{:S(2)}) collective-permute-start(f32[640,640]{1,0:T(8,128)} %parent_last.1), channel_id=1, source_target_pairs={{0,8},{8,0},{16,24},{24,16},{1,9},{9,1},{17,25},{25,17},{2,10},{10... | collective-permute-start | bytes 4915208 | tf_op jit(solution)/shard_map/ppermute | solution.py:314
  188.6 2.1 collective-permute-done.11
  190.7 1.6 broadcast_select_fusion
  192.3 3.0 %collective-permute-start.12 = (f32[640,640]{1,0:T(8,128)S(1)}, f32[640,640]{1,0:T(8,128)S(1)}, u32[]{:S(2)}, u32[]{:S(2)}) collective-permute-start(f32[640,640]{1,0:T(8,128)S(1)} %broadcast_select_fusion), channel_id=1, source_target_pairs={{0,1},{1,0},{2,3},{3,2},{4,5},{5,4},{6,7},{7,6},{8,9},{9,8},{10,11... | collective-permute-start | bytes 4915208 | tf_op jit(solution)/shard_map/ppermute | solution.py:314
  196.0 35.6 %collective-permute-done.12 = f32[640,640]{1,0:T(8,128)S(1)} collective-permute-done((f32[640,640]{1,0:T(8,128)S(1)}, f32[640,640]{1,0:T(8,128)S(1)}, u32[]{:S(2)}, u32[]{:S(2)}) %collective-permute-start.12) | collective-permute-done | bytes 1638432 | tf_op jit(solution)/shard_map/ppermute | solution.py:314
  231.6 1.3 select_bitcast_fusion
  (42 shorter events, 13.6 us)
Async XLA Ops:
  12.6 26.8 %collective-permute-start = (f32[6,160,256]{2,1,0:T(8,128)}, f32[6,160,256]{2,1,0:T(8,128)S(1)}, u32[]{:S(2)}, u32[]{:S(2)}) collective-permute-start(f32[6,160,256]{2,1,0:T(8,128)} %get-tuple-element.27), channel_id=1, source_target_pairs={{1,0},{2,1},{3,2},{4,3},{5,4},{6,5},{7,6},{9,8},{10,9},{11,10},{12... | collective-permute-start | bytes 2949128 | tf_op jit(solution)/shard_map/ppermute | solution.py:309
  13.9 25.5 %collective-permute-start.1 = (f32[6,160,256]{2,1,0:T(8,128)}, f32[6,160,256]{2,1,0:T(8,128)S(1)}, u32[]{:S(2)}, u32[]{:S(2)}) collective-permute-start(f32[6,160,256]{2,1,0:T(8,128)} %get-tuple-element.28), channel_id=1, source_target_pairs={{8,0},{16,8},{24,16},{9,1},{17,9},{25,17},{10,2},{18,10},{26,18},{... | collective-permute-start | bytes 2949128 | tf_op jit(solution)/shard_map/ppermute | solution.py:309
  39.4 0.9 copy-start
  39.4 1.4 copy-start.4
  55.7 8.3 %collective-permute-start.2 = (f32[6,160,256]{2,1,0:T(8,128)}, f32[6,160,256]{2,1,0:T(8,128)S(1)}, u32[]{:S(2)}, u32[]{:S(2)}) collective-permute-start(f32[6,160,256]{2,1,0:T(8,128)} %get-tuple-element.33), channel_id=1, source_target_pairs={{8,0},{16,8},{24,16},{9,1},{17,9},{25,17},{10,2},{18,10},{26,18},{... | collective-permute-start | bytes 2949128 | tf_op jit(solution)/shard_map/ppermute | solution.py:309
  57.0 25.6 %collective-permute-start.3 = (f32[4,160,256]{2,1,0:T(8,128)}, f32[4,160,256]{2,1,0:T(8,128)S(1)}, u32[]{:S(2)}, u32[]{:S(2)}) collective-permute-start(f32[4,160,256]{2,1,0:T(8,128)} %get-tuple-element.35), channel_id=1, source_target_pairs={{0,1},{1,2},{2,3},{3,4},{4,5},{5,6},{6,7},{8,9},{9,10},{10,11},{11... | collective-permute-start | bytes 1966088 | tf_op jit(solution)/shard_map/ppermute | solution.py:309
  62.8 19.9 %collective-permute-start.5 = (f32[4,160,256]{2,1,0:T(8,128)S(1)}, f32[4,160,256]{2,1,0:T(8,128)S(1)}, u32[]{:S(2)}, u32[]{:S(2)}) collective-permute-start(f32[4,160,256]{2,1,0:T(8,128)S(1)} %slice.23), channel_id=1, source_target_pairs={{8,0},{16,8},{24,16},{9,1},{17,9},{25,17},{10,2},{18,10},{26,18},{... | collective-permute-start | bytes 1966088 | tf_op jit(solution)/shard_map/ppermute | solution.py:309
  64.1 2.8 %copy-start.1 = (f32[6,160,256]{2,1,0:T(8,128)}, f32[6,160,256]{2,1,0:T(8,128)S(1)}, u32[]{:S(2)}) copy-start(f32[6,160,256]{2,1,0:T(8,128)S(1)} %collective-permute-done.2.refs_5_) | copy-start | bytes 2949124
  64.2 26.6 %collective-permute-start.4 = (f32[4,160,256]{2,1,0:T(8,128)S(1)}, f32[4,160,256]{2,1,0:T(8,128)S(1)}, u32[]{:S(2)}, u32[]{:S(2)}) collective-permute-start(f32[4,160,256]{2,1,0:T(8,128)S(1)} %bitcast.11), channel_id=1, source_target_pairs={{0,1},{1,2},{2,3},{3,4},{4,5},{5,6},{6,7},{8,9},{9,10},{10,11},{11... | collective-permute-start | bytes 1966088 | tf_op jit(solution)/shard_map/ppermute | solution.py:309
  82.7 8.1 %copy-start.5 = (f32[4,160,256]{2,1,0:T(8,128)}, f32[4,160,256]{2,1,0:T(8,128)S(1)}, u32[]{:S(2)}) copy-start(f32[4,160,256]{2,1,0:T(8,128)S(1)} %collective-permute-done.3.refs_3_.refs_2_) | copy-start | bytes 1966084
  82.7 8.1 %copy-start.6 = (f32[4,160,256]{2,1,0:T(8,128)}, f32[4,160,256]{2,1,0:T(8,128)S(1)}, u32[]{:S(2)}) copy-start(f32[4,160,256]{2,1,0:T(8,128)S(1)} %collective-permute-done.5.refs_5_.refs_1_) | copy-start | bytes 1966084
  90.8 0.8 copy-start.11
  107.3 27.5 %collective-permute-start.6 = (f32[6,160,256]{2,1,0:T(8,128)}, f32[6,160,256]{2,1,0:T(8,128)S(1)}, u32[]{:S(2)}, u32[]{:S(2)}) collective-permute-start(f32[6,160,256]{2,1,0:T(8,128)} %get-tuple-element.39), channel_id=1, source_target_pairs={{1,0},{2,1},{3,2},{4,3},{5,4},{6,5},{7,6},{9,8},{10,9},{11,10},{12... | collective-permute-start | bytes 2949128 | tf_op jit(solution)/shard_map/ppermute | solution.py:309
  108.6 26.2 %collective-permute-start.7 = (f32[2,160,256]{2,1,0:T(8,128)}, f32[2,160,256]{2,1,0:T(8,128)S(1)}, u32[]{:S(2)}, u32[]{:S(2)}) collective-permute-start(f32[2,160,256]{2,1,0:T(8,128)} %get-tuple-element.40), channel_id=1, source_target_pairs={{0,8},{8,16},{16,24},{1,9},{9,17},{17,25},{2,10},{10,18},{18,26},{... | collective-permute-start | bytes 983048 | tf_op jit(solution)/shard_map/ppermute | solution.py:309
  134.7 0.7 copy-start.7
  135.5 1.0 copy-start.3
  151.2 7.4 %collective-permute-start.8 = (f32[4,160,256]{2,1,0:T(8,128)}, f32[4,160,256]{2,1,0:T(8,128)S(1)}, u32[]{:S(2)}, u32[]{:S(2)}) collective-permute-start(f32[4,160,256]{2,1,0:T(8,128)} %get-tuple-element.43), channel_id=1, source_target_pairs={{0,8},{8,16},{16,24},{1,9},{9,17},{17,25},{2,10},{10,18},{18,26},{... | collective-permute-start | bytes 1966088 | tf_op jit(solution)/shard_map/ppermute | solution.py:309
  153.6 22.4 %collective-permute-start.9 = (f32[2,160,256]{2,1,0:T(8,128)}, f32[2,160,256]{2,1,0:T(8,128)S(1)}, u32[]{:S(2)}, u32[]{:S(2)}) collective-permute-start(f32[2,160,256]{2,1,0:T(8,128)} %get-tuple-element.44), channel_id=1, source_target_pairs={{0,1},{1,2},{2,3},{3,4},{4,5},{5,6},{6,7},{8,9},{9,10},{10,11},{11... | collective-permute-start | bytes 983048 | tf_op jit(solution)/shard_map/ppermute | solution.py:309
  158.7 17.4 %copy-start.2 = (f32[4,160,256]{2,1,0:T(8,128)}, f32[4,160,256]{2,1,0:T(8,128)S(1)}, u32[]{:S(2)}) copy-start(f32[4,160,256]{2,1,0:T(8,128)S(1)} %collective-permute-done.8.refs_0_) | copy-start | bytes 1966084
  158.7 17.4 %collective-permute-start.10 = (f32[1,160,256]{2,1,0:T(8,128)S(1)}, f32[1,160,256]{2,1,0:T(8,128)S(1)}, u32[]{:S(2)}, u32[]{:S(2)}) collective-permute-start(f32[1,160,256]{2,1,0:T(8,128)S(1)} %slice.24), channel_id=1, source_target_pairs={{0,1},{1,2},{2,3},{3,4},{4,5},{5,6},{6,7},{8,9},{9,10},{10,11},{11... | collective-permute-start | bytes 491528 | tf_op jit(solution)/shard_map/ppermute | solution.py:309
  176.0 11.3 %copy-start.10 = (s32[1,1,2]{2,1,0:T(1,128)S(1)}, s32[1,1,2]{2,1,0:T(1,128)}, u32[]{:S(2)}) copy-start(s32[1,1,2]{2,1,0:T(1,128)} %param.7) | copy-start | bytes 28
  176.0 0.7 copy-start.8
  184.7 6.0 %collective-permute-start.11 = (f32[640,640]{1,0:T(8,128)}, f32[640,640]{1,0:T(8,128)S(1)}, u32[]{:S(2)}, u32[]{:S(2)}) collective-permute-start(f32[640,640]{1,0:T(8,128)} %parent_last.1), channel_id=1, source_target_pairs={{0,8},{8,0},{16,24},{24,16},{1,9},{9,1},{17,25},{25,17},{2,10},{10... | collective-permute-start | bytes 4915208 | tf_op jit(solution)/shard_map/ppermute | solution.py:314
  192.3 39.3 %collective-permute-start.12 = (f32[640,640]{1,0:T(8,128)S(1)}, f32[640,640]{1,0:T(8,128)S(1)}, u32[]{:S(2)}, u32[]{:S(2)}) collective-permute-start(f32[640,640]{1,0:T(8,128)S(1)} %broadcast_select_fusion), channel_id=1, source_target_pairs={{0,1},{1,0},{2,3},{3,2},{4,5},{5,4},{6,7},{7,6},{8,9},{9,8},{10,11... | collective-permute-start | bytes 4915208 | tf_op jit(solution)/shard_map/ppermute | solution.py:314
  (1 other events, 0.7 us)
where the time goes:
time: 234 us; the launch traced here: 233 us
  Pallas kernels  126 us (54%)
  waiting for transfers between devices  59.7 us (26%)
  starting transfers between devices  35.5 us (15%)
  local copies, waits for them, and re-layouts  7.14 us (3%)
  other arithmetic  2.98 us (1%)
    pallas_call x4, Pallas kernels, eliminate(): pl.pallas_call(functools.partial(eliminate_kernel, home, base_at, plan, r...  57.9 us
    ppermute x2, waiting for transfers between devices, from_partner(): return lax.ppermute(value, axis, pairs)  37.7 us
    pallas_call x3, Pallas kernels, update(): pl.pallas_call(functools.partial(update_kernel, jobs, len(bases), len(sou...  33.7 us
    ppermute x11, starting transfers between devices, send(): return lax.ppermute(value, axis, pairs)  29.9 us
    ppermute x11, waiting for transfers between devices, send(): return lax.ppermute(value, axis, pairs)  22 us
    pallas_call x1, Pallas kernels, local(): pl.pallas_call(functools.partial(parent_early_kernel, [entry[1:] for entr...  14.9 us
    pallas_call x1, Pallas kernels, local(): pl.pallas_call(functools.partial(parent_middle_kernel, [entry[1:] for ent...  12.3 us
    pallas_call x1, Pallas kernels, local(): pl.pallas_call(functools.partial(parent_last_kernel, [entry[1:] for entry...  7.24 us
  transfers between devices with their start and end apart: 13, of which 4 were waited for; matrix products, arithmetic and copies ran while one was open for 1% of the time, Pallas kernels for 26%

commit v1 on v0

v1 whole, which is shorter than its diff:
```python
import functools

import jax
import jax.numpy as jnp
from jax import lax
from jax.experimental import pallas as pl
from jax.experimental.pallas import tpu as pltpu
from jax.sharding import PartitionSpec as P

EXACT = lax.Precision.HIGHEST
GROUP = 8
BLOCK = 32
MESH = pl.DeviceIdType.MESH
LOW_FIRST = (0, -1)

FULL = [(a, e) for a in (-1, 0, 1) for e in (-1, 0, 1)]
TRAVEL = {
    "l0": [(0, -1), (1, 0), (-1, 0), (-1, -1), (1, -1), (0, 0)],
    "u0": [(-1, 0), (-1, -1), (0, -1), (0, 0), (-1, 1), (0, 1)],
    "d0": [(0, -1), (-1, 0), (-1, -1), (0, 0)],
    "r1": [(1, 1), (-1, 1), (-1, 0), (1, 0), (0, 1), (0, 0)],
    "u1": [(-1, -1), (-1, 0), (-1, 1), (0, -1), (0, 0), (0, 1)],
    "d1": [(-1, 1), (-1, 0), (0, 1), (0, 0)],
    "l2": [(0, -1), (-1, 0), (0, 0), (1, 0), (1, -1), (-1, -1)],
    "v2": [(1, 0), (1, 1)],
    "d2": [(1, -1)],
    "r3": [(-1, 1), (0, 1), (1, 1)],
    "v3": [(1, -1), (1, 0)],
    "d3": [(1, 1)],
}
FIRST = {}
COUNT = 0
for _name, _panels in TRAVEL.items():
    FIRST[_name] = COUNT
    COUNT += len(_panels)


def slot(name, k):
    return FIRST[name] + TRAVEL[name].index(k)


def near_at(k):
    return (k[0] + 1) * 3 + k[1] + 1


def split(value):
    high = value.astype(jnp.bfloat16)
    low = (value - high.astype(jnp.float32)).astype(jnp.bfloat16)
    return high, low


def dot(left, right):
    return jnp.dot(left, right, preferred_element_type=jnp.float32)


def diagonal_inverse(block):
    size = block.shape[0]
    rows = lax.broadcasted_iota(jnp.int32, (size, size), 0)
    cols = lax.broadcasted_iota(jnp.int32, (size, size), 1)
    eye = (rows == cols).astype(jnp.float32)
    wide = jnp.concatenate([block, eye, jnp.zeros((size, 128 - 2 * size), jnp.float32)], axis=1)
    row_ids = lax.broadcasted_iota(jnp.int32, (size, 128), 0)
    scale = jnp.ones((size, 128), jnp.float32)
    for start in range(0, size, GROUP):
        columns = [
            jnp.broadcast_to(wide[:, start + q : start + q + 1], (size, 128)) for q in range(GROUP)
        ]
        for q in range(GROUP):
            at = start + q
            pivot = columns[q][at : at + 1, :]
            inverse = 1.0 / pivot
            below = jnp.where(row_ids > at, columns[q], 0.0)
            scale = jnp.where(row_ids == at, lax.rsqrt(pivot), scale)
            wide = wide - below * (wide[at : at + 1, :] * inverse)
            for p in range(q + 1, GROUP):
                columns[p] = columns[p] - below * (columns[p][at : at + 1, :] * inverse)
    return (wide * scale)[:, size : 2 * size]


def factor_inverse(matrix, hooks=()):
    size = matrix.shape[0]
    rows = lax.broadcasted_iota(jnp.int32, (size, size), 0)
    cols = lax.broadcasted_iota(jnp.int32, (size, size), 1)
    rest = matrix
    right = (rows == cols).astype(jnp.float32)
    done = []
    for start in range(0, size, BLOCK):
        inverse = diagonal_inverse(rest[:BLOCK, :BLOCK])
        top_right = jnp.dot(inverse, right[:BLOCK], precision=EXACT)
        done.append(top_right)
        if start + BLOCK < size:
            top = jnp.dot(inverse, rest[:BLOCK, BLOCK:], precision=EXACT)
            top_t = top.T
            rest = rest[BLOCK:, BLOCK:] - jnp.dot(top_t, top, precision=EXACT)
            right = right[BLOCK:] - jnp.dot(top_t, top_right, precision=EXACT)
        for at, hook in hooks:
            if at == start // BLOCK:
                hook()
    return jnp.concatenate(done, axis=0)


def kernel(sizes, near, interp_all, counts, out, store, interp, panels, stacks, arrived, shared,
           pulled, send_sem, recv_sem, load_sem):
    n_row, n_col = sizes
    points, slots = store.shape[-1], interp.shape[-1]
    low = points - slots
    row, col = lax.axis_index("row"), lax.axis_index("col")
    has = {
        "up": row > 0, "down": row < n_row - 1, "left": col > 0, "right": col < n_col - 1,
    }
    where_to = {
        "up": {"row": row - 1, "col": col}, "down": {"row": row + 1, "col": col},
        "left": {"row": row, "col": col - 1}, "right": {"row": row, "col": col + 1},
    }

    loads = [pltpu.make_async_copy(interp_all.at[i // 2, i % 2], interp.at[i], load_sem.at[4 + i])
             for i in range(4)]
    loads = [pltpu.make_async_copy(near.at[i], store.at[i], load_sem.at[i]) for i in range(4)] + loads
    pulls = {}
    for y in range(4):
        for x in range(y):
            for one, two in ((x, y), (y, x)):
                k = near_at((two // 2 - one // 2, two % 2 - one % 2))
                n = len(pulls)
                pulls[one, two] = n, pltpu.make_async_copy(
                    near.at[one, k, pl.ds(low, slots), :], pulled.at[n], load_sem.at[8 + n]
                )
    loads[0].start()
    loads[4].start()
    for i in (1, 5, 2, 6, 3, 7):
        loads[i].start()
    for _, copy in pulls.values():
        copy.start()

    barrier = pltpu.get_barrier_semaphore()
    for way in has:
        @pl.when(has[way])
        def _(way=way):
            pl.semaphore_signal(barrier, inc=1, device_id=where_to[way], device_id_type=MESH)

    sent = []

    def copy_of(name, k, source, way):
        i = slot(name, k)
        return pltpu.make_async_remote_copy(
            src_ref=source, dst_ref=arrived.at[i], send_sem=send_sem.at[i],
            recv_sem=recv_sem.at[i], device_id=where_to[way], device_id_type=MESH,
        )

    def send(name, k, source, way, and_also=None):
        copy = copy_of(name, k, source, way)
        sent.append((copy, way, and_also))
        if and_also is None:
            pl.when(has[way])(copy.start)
        else:
            pl.when(has[way] & has[and_also])(copy.start)

    def make_stack(value, ref):
        high, less = split(value)
        ref[0:slots] = high
        ref[slots : 2 * slots] = high
        ref[2 * slots : 3 * slots] = less
        ref[3 * slots : 4 * slots] = high

    def receive(name, k, stack):
        i = slot(name, k)
        pltpu.make_async_remote_copy(
            src_ref=arrived.at[i], dst_ref=arrived.at[i], send_sem=send_sem.at[i],
            recv_sem=recv_sem.at[i], device_id=where_to["up"], device_id_type=MESH,
        ).wait_recv()
        make_stack(arrived[i], stack.at[near_at(k)])

    def update(x, stack, one, twos):
        for two in twos:
            at = near_at((two[0] - one[0], two[1] - one[1]))
            store[x, at] = store[x, at] - lax.dot_general(
                stack[near_at(one), 0 : 3 * slots], stack[near_at(two), slots : 4 * slots],
                (((0,), (0,)), ((), ())), preferred_element_type=jnp.float32,
            )

    def update_rect(x, stack, one, rows, cols, skip=()):
        base = near_at(one)

        def body(i, carry):
            a = rows[0] + i
            for e in cols:
                two = (a + 1) * 3 + e + 1
                at = (a - one[0] + 1) * 3 + e - one[1] + 1
                store[x, at] = store[x, at] - lax.dot_general(
                    stack[base, 0 : 3 * slots], stack[two, slots : 4 * slots],
                    (((0,), (0,)), ((), ())), preferred_element_type=jnp.float32,
                )
            return carry

        lax.fori_loop(0, len(rows), body, 0)

    def update_parent(x, stack, one, two):
        at = near_at((two[0] - one[0], two[1] - one[1]))
        change = lax.dot_general(
            stack[near_at(one), 0 : 3 * slots], stack[near_at(two), slots : 4 * slots],
            (((0,), (0,)), ((), ())), preferred_element_type=jnp.float32,
        )
        store[x, at, low:] = store[x, at, low:] - change[low:]

    def panel_maker(x, hooks=()):
        red = counts[x // 2, x % 2]
        row_ids = lax.broadcasted_iota(jnp.int32, (slots, slots), 0)
        col_ids = lax.broadcasted_iota(jnp.int32, (slots, slots), 1)
        masked = jnp.where((row_ids < red) & (col_ids + low >= red), interp[x], 0.0)
        wide_rows = lax.broadcasted_iota(jnp.int32, (slots, points), 0)
        wide_cols = lax.broadcasted_iota(jnp.int32, (slots, points), 1)
        reduce = (wide_rows == wide_cols).astype(jnp.float32) - jnp.concatenate(
            [jnp.zeros((slots, low), jnp.float32), masked], axis=1
        )
        reduced = jnp.dot(reduce, store[x, 4], precision=EXACT)
        block = lax.dot_general(reduced, reduce, (((1,), (1,)), ((), ())), precision=EXACT)
        block = jnp.where(
            (row_ids < red) & (col_ids < red), block, (row_ids == col_ids).astype(jnp.float32)
        )
        block = 0.5 * (block + block.T)
        inverse = factor_inverse(block, hooks)
        inverse = jnp.where(col_ids < red, inverse, 0.0)
        whole_high, whole_low = split(jnp.dot(inverse, reduce, precision=EXACT))
        left = jnp.concatenate([whole_high, whole_high, whole_low], axis=1)

        def make(k):
            at = near_at(k)
            high, less = split(store[x, at])
            value = dot(left, jnp.concatenate([high, less, high], axis=0))
            if k == (0, 0):
                value = jnp.where(wide_cols >= red, value, 0.0)
            panels[x, at] = value
            make_stack(value, stacks.at[x % 2, at])

        return make

    def wait_load(i):
        loads[i].wait()
        loads[4 + i].wait()

    mine = [stacks.at[0], stacks.at[1], stacks.at[0], stacks.at[1]]
    from_right, from_down, from_left, other = (shared.at[i] for i in range(4))

    wait_load(0)
    make = panel_maker(0)
    pl.semaphore_wait(barrier, sum(has[way].astype(jnp.int32) for way in has))
    order = TRAVEL["l0"] + [(-1, 1), (0, 1), (1, 1)]
    for k in order:
        make(k)
        if k in TRAVEL["l0"]:
            send("l0", k, panels.at[0, near_at(k)], "left")
        if k in TRAVEL["u0"]:
            send("u0", k, panels.at[0, near_at(k)], "up")
    wait_load(1)
    wait_load(2)
    wait_load(3)
    update_rect(1, mine[0], (0, 1), (-1, 0, 1), (0, 1))
    update_rect(2, mine[0], (1, 0), (0, 1), (-1, 0, 1))
    update_rect(3, mine[0], (1, 1), (0, 1), (0, 1))
    update_parent(0, mine[0], (0, 0), (0, 0))

    @pl.when(has["right"])
    def _():
        receive("l0", (0, -1), from_right)
        update(1, from_right, (0, -1), [(0, -1)])

    send("d0", (0, -1), arrived.at[slot("l0", (0, -1))], "up", "right")
    make = panel_maker(1)
    for k in TRAVEL["l0"][1:]:
        @pl.when(has["right"])
        def _(k=k):
            receive("l0", k, from_right)
            update(1, from_right, (0, -1), [k])

        if k in TRAVEL["d0"]:
            send("d0", k, arrived.at[slot("l0", k)], "up", "right")
        k = (k[0], k[1] + 1)
        make(k)
        send("r1", k, panels.at[1, near_at(k)], "right")
        if k in TRAVEL["u1"]:
            send("u1", k, panels.at[1, near_at(k)], "up")
    for k in ((0, 0), (-1, -1), (0, -1), (1, -1)):
        make(k)
        if k in TRAVEL["r1"]:
            send("r1", k, panels.at[1, near_at(k)], "right")
        if k in TRAVEL["u1"]:
            send("u1", k, panels.at[1, near_at(k)], "up")
    update_rect(2, mine[1], (1, -1), (0, 1), (-1, 0))
    update_rect(3, mine[1], (1, 0), (0, 1), (-1, 0, 1))
    update_parent(0, mine[1], (0, -1), (0, -1))
    update_parent(1, mine[1], (0, 0), (0, -1))
    update_parent(1, mine[1], (0, 0), (0, 0))

    @pl.when(has["down"])
    def _():
        for k in TRAVEL["u0"]:
            receive("u0", k, from_down)
        update_rect(2, from_down, (-1, 0), (-1, 0), (-1, 0, 1))
        update_rect(3, from_down, (-1, 1), (-1, 0), (0, 1))
        receive("u1", (-1, -1), from_down)
        update(2, from_down, (-1, -1), [(-1, -1)])

    @pl.when(has["left"])
    def _():
        receive("r1", (1, 1), from_left)
        update(2, from_left, (1, 1), [(1, 1)])
        receive("r1", (-1, 1), from_left)

    send("d1", (-1, 1), arrived.at[slot("r1", (-1, 1))], "up", "left")

    @pl.when(has["right"])
    def _():
        update_rect(3, from_right, (1, -1), (0, 1), (-1, 0))

    @pl.when(has["down"] & has["left"])
    def _():
        receive("d1", (-1, 1), other)
        update(2, other, (-1, 1), [(-1, 1)])

    def forward():
        k = (-1, 0)
        pl.when(has["left"])(lambda: receive("r1", k, from_left))
        send("d1", k, arrived.at[slot("r1", k)], "up", "left")

    make = panel_maker(2, [(3, forward)])

    @pl.when(has["down"])
    def _():
        for k in TRAVEL["u1"][1:]:
            receive("u1", k, from_down)
        update(2, from_down, (-1, -1), [(-1, 0), (0, -1), (0, 0)])
        update_rect(3, from_down, (-1, 0), (-1, 0), (-1, 0, 1))

    @pl.when(has["left"])
    def _():
        receive("r1", (1, 0), from_left)
        update(2, from_left, (1, 1), [(1, 0)])

    @pl.when(has["down"] & has["left"])
    def _():
        receive("d1", (-1, 0), other)
        update(2, other, (-1, 1), [(-1, 0)])

    def finish(k):
        make(k)
        if k in TRAVEL["l2"]:
            send("l2", k, panels.at[2, near_at(k)], "left")
        if k in TRAVEL["v2"]:
            send("v2", k, panels.at[2, near_at(k)], "down")

    finish((0, -1))
    finish((0, 0))
    finish((0, 1))
    for k, one, two in (((0, 1), (-1, 0), (1, 0)), ((0, 0), (-1, -1), (1, -1))):
        @pl.when(has["left"])
        def _(k=k):
            receive("r1", k, from_left)
            update(2, from_left, (1, 1), [k])

        send("d1", k, arrived.at[slot("r1", k)], "up", "left")
        finish(one)

        @pl.when(has["down"] & has["left"])
        def _(k=k):
            receive("d1", k, other)
            update(2, other, (-1, 1), [k])

        finish(two)
    finish((1, 1))
    finish((-1, 1))
    update_rect(3, mine[2], (0, 1), (-1, 0, 1), (0, 1))

    @pl.when(has["left"])
    def _():
        update_parent(0, from_left, (0, 1), (0, 1))

    @pl.when(has["down"] & has["right"])
    def _():
        for k in TRAVEL["d0"]:
            receive("d0", k, other)
        update_rect(3, other, (-1, -1), (-1, 0), (-1, 0))

    @pl.when(has["right"])
    def _():
        receive("l2", (0, -1), from_right)
        update(3, from_right, (0, -1), [(0, -1)])

    make = panel_maker(3)
    update_parent(0, mine[2], (-1, 0), (-1, 0))
    update_parent(1, mine[2], (-1, 1), (-1, 0))
    update_parent(1, mine[2], (-1, 1), (-1, 1))
    update_parent(2, mine[2], (0, 0), (-1, 0))
    update_parent(2, mine[2], (0, 0), (-1, 1))
    update_parent(2, mine[2], (0, 0), (0, 0))
    for k in TRAVEL["l2"][1:]:
        @pl.when(has["right"])
        def _(k=k):
            receive("l2", k, from_right)
            update(3, from_right, (0, -1), [k])

        if k in TRAVEL["d2"]:
            send("d2", k, arrived.at[slot("l2", k)], "down", "right")
        k = (k[0], k[1] + 1)
        make(k)
        if k in TRAVEL["r3"]:
            send("r3", k, panels.at[3, near_at(k)], "right")
        if k in TRAVEL["v3"]:
            send("v3", k, panels.at[3, near_at(k)], "down")
    for k in ((1, -1), (0, 0), (-1, -1), (0, -1)):
        make(k)
        if k in TRAVEL["v3"]:
            send("v3", k, panels.at[3, near_at(k)], "down")

    places = [(-1, -1), (-1, 0), (0, -1), (0, 0)]
    for x in range(4):
        for y in range(x + 1):
            update_parent(x, mine[3], places[x], places[y])

    @pl.when(has["right"])
    def _():
        update_parent(1, from_right, (-1, -1), (-1, -1))

    @pl.when(has["up"])
    def _():
        receive("v2", (1, 0), from_down)
        receive("v2", (1, 1), from_down)
        update_parent(0, from_down, (1, 0), (1, 0))
        update_parent(1, from_down, (1, 1), (1, 0))
        update_parent(1, from_down, (1, 1), (1, 1))

    @pl.when(has["up"] & has["right"])
    def _():
        receive("d2", (1, -1), other)
        update_parent(1, other, (1, -1), (1, -1))

    def keep(x, y):
        row_ids = lax.broadcasted_iota(jnp.int32, (slots, slots), 0) + low
        col_ids = lax.broadcasted_iota(jnp.int32, (slots, slots), 1) + low
        return (row_ids >= counts[x // 2, x % 2]) & (col_ids >= counts[y // 2, y % 2])

    for _, copy in pulls.values():
        copy.wait()

    @pl.when(has["left"])
    def _():
        for k in TRAVEL["r3"]:
            receive("r3", k, from_left)

    send("d3", (1, 1), arrived.at[slot("r3", (1, 1))], "down", "left")

    @pl.when(has["left"])
    def _():
        update_parent(0, from_left, (-1, 1), (-1, 1))
        update_parent(2, from_left, (0, 1), (-1, 1))
        update_parent(2, from_left, (0, 1), (0, 1))

    @pl.when(has["up"])
    def _():
        receive("v3", (1, -1), from_down)
        receive("v3", (1, 0), from_down)
        update_parent(0, from_down, (1, -1), (1, -1))
        update_parent(1, from_down, (1, 0), (1, -1))
        update_parent(1, from_down, (1, 0), (1, 0))

    @pl.when(has["up"] & has["left"])
    def _():
        receive("d3", (1, 1), other)
        update_parent(0, other, (1, 1), (1, 1))

    for x in range(4):
        for y in range(x + 1):
            at = near_at((y // 2 - x // 2, y % 2 - x % 2))
            block = jnp.where(keep(x, y), store[x, at, low:][:, low:], 0.0)
            out[x * slots : (x + 1) * slots, y * slots : (y + 1) * slots] = block
            if y < x:
                skew = pulled[pulls[y, x][0]][:, low:] - pulled[pulls[x, y][0]][:, low:].T
                out[y * slots : (y + 1) * slots, x * slots : (x + 1) * slots] = (
                    jnp.where(keep(y, x), skew, 0.0) + block.T
                )
    for copy, way, and_also in sent:
        if and_also is None:
            pl.when(has[way])(copy.wait_send)
        else:
            pl.when(has[way] & has[and_also])(copy.wait_send)


def from_partner(value, axis):
    pairs = [(source, source ^ 1) for source in range(lax.axis_size(axis))]
    return lax.ppermute(value, axis, pairs)


def local(near, interp, red_count, owner_flip):
    points, slots = near.shape[-1], interp.shape[-1]
    boxes = near.reshape(4, 9, points, points)
    any_space = pl.BlockSpec(memory_space=pl.ANY)
    parent = pl.pallas_call(
        functools.partial(kernel, (lax.axis_size("row"), lax.axis_size("col"))),
        out_shape=jax.ShapeDtypeStruct((4 * slots, 4 * slots), jnp.float32),
        in_specs=[any_space, any_space, pl.BlockSpec(memory_space=pltpu.SMEM)],
        out_specs=pl.BlockSpec(memory_space=pltpu.VMEM),
        scratch_shapes=[
            pltpu.VMEM((4, 9, points, points), jnp.float32),
            pltpu.VMEM((4, slots, slots), jnp.float32),
            pltpu.VMEM((4, 9, slots, points), jnp.float32),
            pltpu.VMEM((2, 9, 4 * slots, points), jnp.bfloat16),
            pltpu.VMEM((COUNT, slots, points), jnp.float32),
            pltpu.VMEM((4, 9, 4 * slots, points), jnp.bfloat16),
            pltpu.VMEM((12, slots, points), jnp.float32),
            pltpu.SemaphoreType.DMA((COUNT,)),
            pltpu.SemaphoreType.DMA((COUNT,)),
            pltpu.SemaphoreType.DMA((20,)),
        ],
        compiler_params=pltpu.CompilerParams(
            vmem_limit_bytes=60 * 2**20, collective_id=0, has_side_effects=True
        ),
        name="skeletonize",
    )(boxes, interp, red_count)
    flip = owner_flip[0, 0]
    parent = jnp.where(flip[0] == 1, from_partner(parent, "row"), parent)
    parent = jnp.where(flip[1] == 1, from_partner(parent, "col"), parent)
    return parent[None, None]


def solution(mesh):
    in_specs = (
        P("row", "col", None, None, None, None),
        P("row", "col", None, None),
        P("row", "col"),
        P("row", "col", None),
    )
    out_specs = P("row", "col", None, None)
    return jax.shard_map(local, mesh=mesh, in_specs=in_specs, out_specs=out_specs, check_vma=False)
```

time: 234 us -> 165 us (0.71)
  the two profiles are of different devices: /device:TPU:0 before, /device:TPU:22 now
where the time goes in v1:
time: 165 us
  Pallas kernels  122 us (74%)
  waiting for transfers between devices  39.6 us (24%)
    pallas_call x1, Pallas kernels, local(): pl.pallas_call(functools.partial(kernel, (lax.axis_size('row'), lax.axis_...  122 us
    ppermute x2, waiting for transfers between devices, from_partner(): return lax.ppermute(value, axis, pairs)  39.6 us
  transfers between devices with their start and end apart: 2, of which 2 were waited for; matrix products, arithmetic and copies ran while one was open for 0% of the time, Pallas kernels for 0%

profile of v1, /device:TPU:22, one launch (start us, length us, event | category | flops | bytes accessed | tf_op | source)
XLA Modules:
  0.0 165.1 jit_solution(1293792494077624861)
XLA Ops:
  0.0 0.0 copy-start
  0.0 121.8 %skeletonize.1 = f32[640,640]{1,0:T(8,128)} custom-call(f32[4,9,256,256]{3,2,1,0:T(8,128)} %bitcast.5, f32[2,2,160,160]{3,2,1,0:T(8,128)} %interp_all.1, s32[2,2]{1,0:T(2,128)} %counts.1), custom_call_target="tpu_custom_call" | custom-call | tf_op jit(solution)/shard_map/skeletonize/pallas_call | solution.py:496
  121.8 0.1 collective-permute-start
  121.9 0.0 copy-done
  121.9 0.6 fusion
  123.2 2.4 %collective-permute-done = f32[640,640]{1,0:T(8,128)S(1)} collective-permute-done((f32[640,640]{1,0:T(8,128)}, f32[640,640]{1,0:T(8,128)S(1)}, u32[]{:S(2)}, u32[]{:S(2)}) %collective-permute-start) | collective-permute-done | bytes 1638432 | tf_op jit(solution)/shard_map/ppermute | solution.py:489
  125.6 0.2 broadcast_select_fusion
  125.8 0.1 collective-permute-start.1
  126.6 37.2 %collective-permute-done.1 = f32[640,640]{1,0:T(8,128)S(1)} collective-permute-done((f32[640,640]{1,0:T(8,128)S(1)}, f32[640,640]{1,0:T(8,128)S(1)}, u32[]{:S(2)}, u32[]{:S(2)}) %collective-permute-start.1) | collective-permute-done | bytes 1638432 | tf_op jit(solution)/shard_map/ppermute | solution.py:489
  163.7 1.3 select_bitcast_fusion
Async XLA Ops:
  0.0 121.9 %copy-start = (s32[1,1,2]{2,1,0:T(1,128)S(1)}, s32[1,1,2]{2,1,0:T(1,128)}, u32[]{:S(2)}) copy-start(s32[1,1,2]{2,1,0:T(1,128)} %param.7) | copy-start | bytes 28
  121.8 3.8 %collective-permute-start = (f32[640,640]{1,0:T(8,128)}, f32[640,640]{1,0:T(8,128)S(1)}, u32[]{:S(2)}, u32[]{:S(2)}) collective-permute-start(f32[640,640]{1,0:T(8,128)} %skeletonize.1), channel_id=1, source_target_pairs={{0,8},{8,0},{16,24},{24,16},{1,9},{9,1},{17,25},{25,17},{2,10},{10... | collective-permute-start | bytes 4915208 | tf_op jit(solution)/shard_map/ppermute | solution.py:489
  125.8 37.9 %collective-permute-start.1 = (f32[640,640]{1,0:T(8,128)S(1)}, f32[640,640]{1,0:T(8,128)S(1)}, u32[]{:S(2)}, u32[]{:S(2)}) collective-permute-start(f32[640,640]{1,0:T(8,128)S(1)} %broadcast_select_fusion), channel_id=1, source_target_pairs={{0,1},{1,0},{2,3},{3,2},{4,5},{5,4},{6,7},{7,6},{8,9},{9,8},{10,11... | collective-permute-start | bytes 4915208 | tf_op jit(solution)/shard_map/ppermute | solution.py:489

commit v2 on v1

v2 whole, which is shorter than its diff:
```python
import functools

import jax
import jax.numpy as jnp
from jax import lax
from jax.experimental import pallas as pl
from jax.experimental.pallas import tpu as pltpu
from jax.sharding import PartitionSpec as P

EXACT = lax.Precision.HIGHEST
GROUP = 8
BLOCK = 32
MESH = pl.DeviceIdType.MESH

FULL = [(a, e) for a in (-1, 0, 1) for e in (-1, 0, 1)]
TRAVEL = {
    "l0": [(0, -1), (1, 0), (-1, 0), (-1, -1), (1, -1), (0, 0)],
    "u0": [(-1, 0), (-1, -1), (0, -1), (0, 0), (-1, 1), (0, 1)],
    "d0": [(0, -1), (-1, 0), (-1, -1), (0, 0)],
    "r1": [(1, 1), (-1, 1), (-1, 0), (1, 0), (0, 1), (0, 0)],
    "u1": [(-1, -1), (-1, 0), (-1, 1), (0, -1), (0, 0), (0, 1)],
    "d1": [(-1, 1), (-1, 0), (0, 1), (0, 0)],
    "l2": [(0, -1), (0, 0), (-1, 0), (1, 0), (-1, -1), (1, -1)],
    "v2": [(1, 0), (1, 1)],
    "d2": [(1, -1)],
    "r3": [(-1, 1), (0, 1), (1, 1)],
    "v3": [(1, -1), (1, 0)],
    "d3": [(1, 1)],
}
FIRST = {}
COUNT = 0
for _name, _panels in TRAVEL.items():
    FIRST[_name] = COUNT
    COUNT += len(_panels)


STRIPS = {
    "A3": [(3, 0), (3, 1), (3, 2), (3, 3)],
    "A2": [(2, 0), (2, 1), (2, 2), (0, 0)],
    "A1": [(1, 0), (1, 1)],
    "E3": [(0, 3), (1, 3), (2, 3), (0, 1)],
    "E2": [(0, 2), (1, 2)],
}


def strip_places(slots):
    places, total = {}, 0
    for name, blocks in STRIPS.items():
        width = -(-len(blocks) * slots // 128) * 128
        places[name] = (total, width)
        total += width
    return places, total


PACKED = {("l0", (0, 0)), ("r1", (0, 1)), ("r1", (0, 0)), ("d0", (0, 0)), ("d1", (0, 1)), ("d1", (0, 0))}
PACKED |= {(name, k) for name in ("l2", "r3", "d2", "d3") for k in TRAVEL[name]} - {("l2", (0, -1))}
PACKED = sorted(PACKED)


def slot(name, k):
    return FIRST[name] + TRAVEL[name].index(k)


def near_at(k):
    return (k[0] + 1) * 3 + k[1] + 1


def split(value):
    high = value.astype(jnp.bfloat16)
    low = (value - high.astype(jnp.float32)).astype(jnp.bfloat16)
    return high, low


def dot(left, right):
    return jnp.dot(left, right, preferred_element_type=jnp.float32)


def diagonal_inverse(block):
    size = block.shape[0]
    rows = lax.broadcasted_iota(jnp.int32, (size, size), 0)
    cols = lax.broadcasted_iota(jnp.int32, (size, size), 1)
    eye = (rows == cols).astype(jnp.float32)
    wide = jnp.concatenate([block, eye, jnp.zeros((size, 128 - 2 * size), jnp.float32)], axis=1)
    row_ids = lax.broadcasted_iota(jnp.int32, (size, 128), 0)
    scale = jnp.ones((size, 128), jnp.float32)
    for start in range(0, size, GROUP):
        columns = [
            jnp.broadcast_to(wide[:, start + q : start + q + 1], (size, 128)) for q in range(GROUP)
        ]
        for q in range(GROUP):
            at = start + q
            pivot = columns[q][at : at + 1, :]
            inverse = 1.0 / pivot
            below = jnp.where(row_ids > at, columns[q], 0.0)
            scale = jnp.where(row_ids == at, lax.rsqrt(pivot), scale)
            wide = wide - below * (wide[at : at + 1, :] * inverse)
            for p in range(q + 1, GROUP):
                columns[p] = columns[p] - below * (columns[p][at : at + 1, :] * inverse)
    return (wide * scale)[:, size : 2 * size]


def factor_inverse(matrix, hooks=()):
    size = matrix.shape[0]
    rows = lax.broadcasted_iota(jnp.int32, (size, size), 0)
    cols = lax.broadcasted_iota(jnp.int32, (size, size), 1)
    rest = matrix
    right = (rows == cols).astype(jnp.float32)
    done = []
    for start in range(0, size, BLOCK):
        inverse = diagonal_inverse(rest[:BLOCK, :BLOCK])
        top_right = jnp.dot(inverse, right[:BLOCK], precision=EXACT)
        done.append(top_right)
        if start + BLOCK < size:
            top = jnp.dot(inverse, rest[:BLOCK, BLOCK:], precision=EXACT)
            top_t = top.T
            rest = rest[BLOCK:, BLOCK:] - jnp.dot(top_t, top, precision=EXACT)
            right = right[BLOCK:] - jnp.dot(top_t, top_right, precision=EXACT)
        for at, hook in hooks:
            if at == start // BLOCK:
                hook()
    return jnp.concatenate(done, axis=0)


def kernel(sizes, near, interp_all, counts, flip, out, store, interp, panels, tops, stacks, arrived,
           packed, small, shared, pulled, own, first_got, chosen, last_got, send_sem, recv_sem, load_sem, strip_send,
           strip_recv):
    n_row, n_col = sizes
    points, slots = store.shape[-1], interp.shape[-1]
    low = points - slots
    row, col = lax.axis_index("row"), lax.axis_index("col")
    has = {
        "up": row > 0, "down": row < n_row - 1, "left": col > 0, "right": col < n_col - 1,
    }
    where_to = {
        "up": {"row": row - 1, "col": col}, "down": {"row": row + 1, "col": col},
        "left": {"row": row, "col": col - 1}, "right": {"row": row, "col": col + 1},
    }
    row_partner = {"row": row + 1 - 2 * lax.rem(row, 2), "col": col}
    col_partner = {"row": row, "col": col + 1 - 2 * lax.rem(col, 2)}

    loads = [pltpu.make_async_copy(near.at[i], store.at[i], load_sem.at[i]) for i in range(4)]
    loads += [
        pltpu.make_async_copy(interp_all.at[i // 2, i % 2], interp.at[i], load_sem.at[4 + i])
        for i in range(4)
    ]
    pulls = {}
    for y in range(4):
        for x in range(y):
            for one, two in ((x, y), (y, x)):
                k = near_at((two // 2 - one // 2, two % 2 - one % 2))
                n = len(pulls)
                pulls[one, two] = n, pltpu.make_async_copy(
                    near.at[one, k, pl.ds(low, slots), :], pulled.at[n], load_sem.at[8 + n]
                )
    for _, copy in pulls.values():
        copy.start()
    for i in (0, 4, 1, 5, 2, 6, 3, 7):
        loads[i].start()

    barrier = pltpu.get_barrier_semaphore()
    for way in has:
        @pl.when(has[way])
        def _(way=way):
            pl.semaphore_signal(barrier, inc=1, device_id=where_to[way], device_id_type=MESH)

    sent = []

    lanes = points // 2
    tail = points - low - lanes
    piece = slots * tail // lanes

    def pack(value, ref):
        ref[0:slots] = value[:, lanes:]
        lane_ids = lax.broadcasted_iota(jnp.int32, (piece, lanes), 1)
        folded = jnp.zeros((piece, lanes), jnp.float32)
        for i in range(slots // piece):
            part = pltpu.roll(value[i * piece : (i + 1) * piece, :lanes], (i * tail - low) % lanes, 1)
            inside = (lane_ids >= i * tail) & (lane_ids < (i + 1) * tail)
            folded = jnp.where(inside, part, folded)
        ref[slots:] = folded

    def unpack(ref):
        parts = [pltpu.roll(ref[slots:], (low - i * tail) % lanes, 1) for i in range(slots // piece)]
        front = jnp.concatenate(parts, axis=0)
        lane_ids = lax.broadcasted_iota(jnp.int32, (slots, lanes), 1)
        return jnp.concatenate([jnp.where(lane_ids >= low, front, 0.0), ref[0:slots]], axis=1)

    def landing(name, k):
        if (name, k) in PACKED:
            return small.at[PACKED.index((name, k))]
        return arrived.at[slot(name, k)]

    def copy_of(name, k, source, way):
        i = slot(name, k)
        return pltpu.make_async_remote_copy(
            src_ref=source, dst_ref=landing(name, k), send_sem=send_sem.at[i],
            recv_sem=recv_sem.at[i], device_id=where_to[way], device_id_type=MESH,
        )

    def send(name, k, source, way, and_also=None):
        if source is None:
            source = panels.at[int(name[1]), near_at(k)]
            if (name, k) in PACKED:
                staged = packed.at[PACKED.index((name, k))]
                pl.when(has[way])(lambda: pack(source[...], staged))
                source = staged
        copy = copy_of(name, k, source, way)
        sent.append((copy, way, and_also))
        if and_also is None:
            pl.when(has[way])(copy.start)
        else:
            pl.when(has[way] & has[and_also])(copy.start)

    def make_stack(value, ref):
        high, less = split(value)
        ref[0:slots] = high
        ref[slots : 2 * slots] = high
        ref[2 * slots : 3 * slots] = less
        ref[3 * slots : 4 * slots] = high

    def arrive(name, k):
        i = slot(name, k)
        pltpu.make_async_remote_copy(
            src_ref=landing(name, k), dst_ref=landing(name, k), send_sem=send_sem.at[i],
            recv_sem=recv_sem.at[i], device_id=where_to["up"], device_id_type=MESH,
        ).wait_recv()
        return unpack(landing(name, k)) if (name, k) in PACKED else arrived[i]

    def receive(name, k, stack):
        make_stack(arrive(name, k), stack.at[near_at(k)])

    def product(stack, one, two):
        return lax.dot_general(
            stack[near_at(one), 0 : 3 * slots], stack[near_at(two), slots : 4 * slots],
            (((0,), (0,)), ((), ())), preferred_element_type=jnp.float32,
        )

    def update(x, stack, one, twos):
        for two in twos:
            at = near_at((two[0] - one[0], two[1] - one[1]))
            store[x, at] = store[x, at] - product(stack, one, two)

    def update_rect(x, stack, one, rows, cols):
        base = near_at(one)

        def body(i, carry):
            a = rows[0] + i
            for e in cols:
                two = (a + 1) * 3 + e + 1
                at = (a - one[0] + 1) * 3 + e - one[1] + 1
                store[x, at] = store[x, at] - lax.dot_general(
                    stack[base, 0 : 3 * slots], stack[two, slots : 4 * slots],
                    (((0,), (0,)), ((), ())), preferred_element_type=jnp.float32,
                )
            return carry

        lax.fori_loop(0, len(rows), body, 0)

    def update_parent(x, stack, one, two):
        at = near_at((two[0] - one[0], two[1] - one[1]))
        store[x, at, low:] = store[x, at, low:] - product(stack, one, two)[low:]

    def panel_maker(x, hooks=()):
        red = counts[x // 2, x % 2]
        row_ids = lax.broadcasted_iota(jnp.int32, (slots, slots), 0)
        col_ids = lax.broadcasted_iota(jnp.int32, (slots, slots), 1)
        masked = jnp.where((row_ids < red) & (col_ids + low >= red), interp[x], 0.0)
        wide_rows = lax.broadcasted_iota(jnp.int32, (slots, points), 0)
        wide_cols = lax.broadcasted_iota(jnp.int32, (slots, points), 1)
        reduce = (wide_rows == wide_cols).astype(jnp.float32) - jnp.concatenate(
            [jnp.zeros((slots, low), jnp.float32), masked], axis=1
        )
        reduced = jnp.dot(reduce, store[x, 4], precision=EXACT)
        block = lax.dot_general(reduced, reduce, (((1,), (1,)), ((), ())), precision=EXACT)
        block = jnp.where(
            (row_ids < red) & (col_ids < red), block, (row_ids == col_ids).astype(jnp.float32)
        )
        block = 0.5 * (block + block.T)
        inverse = factor_inverse(block, hooks)
        inverse = jnp.where(col_ids < red, inverse, 0.0)
        whole_high, whole_low = split(jnp.dot(inverse, reduce, precision=EXACT))
        tops[x] = jnp.concatenate([whole_high, whole_high, whole_low], axis=1)

        def make(k):
            at = near_at(k)
            high, less = split(store[x, at])
            value = dot(tops[x], jnp.concatenate([high, less, high], axis=0))
            if k == (0, 0):
                value = jnp.where(wide_cols >= red, value, 0.0)
            panels[x, at] = value
            make_stack(value, stacks.at[x % 2, at])

        return make

    def keep(x, y):
        row_ids = lax.broadcasted_iota(jnp.int32, (slots, slots), 0) + low
        col_ids = lax.broadcasted_iota(jnp.int32, (slots, slots), 1) + low
        return (row_ids >= counts[x // 2, x % 2]) & (col_ids >= counts[y // 2, y % 2])

    places, _ = strip_places(slots)
    strip_at = list(STRIPS)

    def strip_copy(name, first_hop):
        along_row = first_hop == (name[0] == "A")
        i = strip_at.index(name) + (0 if first_hop else len(strip_at))
        first, width = places[name]
        source, target = (own, first_got) if first_hop else (chosen, last_got)
        return pltpu.make_async_remote_copy(
            src_ref=source.at[:, pl.ds(first, width)], dst_ref=target.at[:, pl.ds(first, width)],
            send_sem=strip_send.at[i], recv_sem=strip_recv.at[i],
            device_id=row_partner if along_row else col_partner, device_id_type=MESH,
        )

    def pick(name, first_hop):
        first, width = places[name]
        view = (slice(None), slice(first, first + width))
        axis = 0 if first_hop == (name[0] == "A") else 1
        flipped = jnp.full((slots, width), flip[0, 0, axis], jnp.int32) == 1
        if first_hop:
            return jnp.where(flipped, first_got[view], own[view])
        return jnp.where(flipped, last_got[view], chosen[view])

    def start_strip(name):
        for at, (x, y) in enumerate(STRIPS[name]):
            first = places[name][0] + at * slots
            at = near_at((y // 2 - x // 2, y % 2 - x % 2))
            if name[0] == "A":
                block = store[x, at, low:][:, low:]
            else:
                block = pulled[pulls[x, y][0]][:, low:] - pulled[pulls[y, x][0]][:, low:].T
            own[:, first : first + slots] = jnp.where(keep(x, y), block, 0.0)
        end = places[name][0] + len(STRIPS[name]) * slots
        if end < sum(places[name]):
            own[:, end : sum(places[name])] = jnp.zeros((slots, sum(places[name]) - end), jnp.float32)
        strip_copy(name, True).start()

    def pass_strip(name):
        strip_copy(name, True).wait_recv()
        first, width = places[name]
        chosen[:, first : first + width] = pick(name, True)
        strip_copy(name, False).start()

    def end_strip(name):
        strip_copy(name, False).wait_recv()
        value = pick(name, False)
        for at, (x, y) in enumerate(STRIPS[name]):
            block = value[:, at * slots : (at + 1) * slots]
            rows, cols = slice(x * slots, (x + 1) * slots), slice(y * slots, (y + 1) * slots)
            out[rows, cols] = block
            if name[0] == "A" and y < x:
                out[cols, rows] = out[cols, rows] + block.T

    def wait_load(i):
        loads[i].wait()
        loads[4 + i].wait()

    mine = [stacks.at[0], stacks.at[1], stacks.at[0], stacks.at[1]]
    from_right, from_down, from_left, other = (shared.at[i] for i in range(4))

    for _, copy in pulls.values():
        copy.wait()
    pl.semaphore_wait(barrier, sum(has[way].astype(jnp.int32) for way in has))
    start_strip("E3")
    wait_load(0)
    make = panel_maker(0)
    for k in TRAVEL["l0"] + [(-1, 1), (0, 1), (1, 1)]:
        make(k)
        if k in TRAVEL["l0"]:
            send("l0", k, None, "left")
        if k in TRAVEL["u0"]:
            send("u0", k, None, "up")
    wait_load(1)
    wait_load(2)
    wait_load(3)
    update_rect(1, mine[0], (0, 1), (-1, 0, 1), (0, 1))
    update_rect(2, mine[0], (1, 0), (0, 1), (-1, 0, 1))
    update_rect(3, mine[0], (1, 1), (0, 1), (0, 1))
    update_parent(0, mine[0], (0, 0), (0, 0))

    @pl.when(has["right"])
    def _():
        receive("l0", (0, -1), from_right)
        update(1, from_right, (0, -1), [(0, -1)])

    send("d0", (0, -1), landing("l0", (0, -1)), "up", "right")
    make_one = panel_maker(1)

    def finish_one(k):
        make_one(k)
        if k in TRAVEL["r1"]:
            send("r1", k, None, "right")
        if k in TRAVEL["u1"]:
            send("u1", k, None, "up")

    def step_one(k):
        @pl.when(has["right"])
        def _():
            receive("l0", k, from_right)
            update(1, from_right, (0, -1), [k])

        if k in TRAVEL["d0"]:
            send("d0", k, landing("l0", k), "up", "right")
        finish_one((k[0], k[1] + 1))

    step_one((1, 0))
    step_one((-1, 0))
    finish_one((-1, -1))
    finish_one((1, -1))
    finish_one((0, -1))
    update(2, mine[1], (1, -1), [(1, -1), (0, -1)])
    update_parent(0, mine[1], (0, -1), (0, -1))

    @pl.when(has["down"])
    def _():
        for k in TRAVEL["u0"]:
            receive("u0", k, from_down)
        update_rect(2, from_down, (-1, 0), (-1, 0), (-1, 0, 1))
        update_rect(3, from_down, (-1, 1), (-1, 0), (0, 1))
        receive("u1", (-1, -1), from_down)
        update(2, from_down, (-1, -1), [(-1, -1)])

    @pl.when(has["left"])
    def _():
        receive("r1", (1, 1), from_left)
        update(2, from_left, (1, 1), [(1, 1)])
        arrive("r1", (-1, 1))

    send("d1", (-1, 1), landing("r1", (-1, 1)), "up", "left")

    @pl.when(has["down"] & has["left"])
    def _():
        receive("d1", (-1, 1), other)
        update(2, other, (-1, 1), [(-1, 1)])

    def pass_on(k):
        pl.when(has["left"])(lambda: receive("r1", k, from_left))
        send("d1", k, landing("r1", k), "up", "left")

    def last_one():
        step_one((0, 0))
        finish_one((0, 0))

    make_two = panel_maker(2, [
        (0, lambda: step_one((-1, -1))), (1, lambda: step_one((1, -1))), (2, last_one),
        (3, lambda: pass_on((-1, 0))),
    ])

    @pl.when(has["left"])
    def _():
        receive("r1", (1, 0), from_left)
        update(2, from_left, (1, 1), [(1, 0)])

    @pl.when(has["down"] & has["left"])
    def _():
        receive("d1", (-1, 0), other)
        update(2, other, (-1, 1), [(-1, 0)])

    def finish_two(k):
        make_two(k)
        if k in TRAVEL["l2"]:
            send("l2", k, None, "left")
        if k in TRAVEL["v2"]:
            send("v2", k, None, "down")

    finish_two((0, -1))
    finish_two((0, 0))
    pass_on((0, 1))

    @pl.when(has["left"])
    def _():
        update(2, from_left, (1, 1), [(0, 1)])

    finish_two((-1, 0))

    @pl.when(has["down"])
    def _():
        for k in TRAVEL["u1"][1:]:
            receive("u1", k, from_down)
        update(2, from_down, (-1, -1), [(-1, 0), (0, -1), (0, 0)])

    update(2, mine[1], (1, -1), [(1, 0), (0, 0)])
    pass_on((0, 0))

    @pl.when(has["down"] & has["left"])
    def _():
        receive("d1", (0, 1), other)
        update(2, other, (-1, 1), [(0, 1)])

    finish_two((1, 0))

    @pl.when(has["left"])
    def _():
        update(2, from_left, (1, 1), [(0, 0)])
        update_parent(0, from_left, (0, 1), (0, 1))

    finish_two((-1, -1))

    @pl.when(has["down"] & has["left"])
    def _():
        receive("d1", (0, 0), other)
        update(2, other, (-1, 1), [(0, 0)])

    finish_two((1, -1))
    finish_two((1, 1))
    finish_two((0, 1))
    finish_two((-1, 1))
    update_rect(3, mine[2], (0, 1), (-1, 0, 1), (0, 1))
    update_rect(3, mine[1], (1, 0), (0, 1), (-1, 0, 1))
    update_parent(1, mine[1], (0, 0), (0, -1))
    update_parent(1, mine[1], (0, 0), (0, 0))

    @pl.when(has["right"])
    def _():
        update_rect(3, from_right, (1, -1), (0, 1), (-1, 0))

    @pl.when(has["down"])
    def _():
        update_rect(3, from_down, (-1, 0), (-1, 0), (-1, 0, 1))

    @pl.when(has["down"] & has["right"])
    def _():
        for k in TRAVEL["d0"]:
            receive("d0", k, other)
        update_rect(3, other, (-1, -1), (-1, 0), (-1, 0))

    @pl.when(has["right"])
    def _():
        receive("l2", (0, -1), from_right)
        update(3, from_right, (0, -1), [(0, -1)])

    start_strip("E2")
    make_three = panel_maker(3)
    pass_strip("E3")
    update_parent(0, mine[2], (-1, 0), (-1, 0))
    update_parent(1, mine[2], (-1, 1), (-1, 0))
    update_parent(1, mine[2], (-1, 1), (-1, 1))
    update_parent(2, mine[2], (0, 0), (-1, 0))
    update_parent(2, mine[2], (0, 0), (-1, 1))
    update_parent(2, mine[2], (0, 0), (0, 0))
    end_strip("E3")

    def finish_three(k):
        make_three(k)
        if k in TRAVEL["r3"]:
            send("r3", k, None, "right")
        if k in TRAVEL["v3"]:
            send("v3", k, None, "down")

    for k in TRAVEL["l2"][1:]:
        @pl.when(has["right"])
        def _(k=k):
            receive("l2", k, from_right)
            update(3, from_right, (0, -1), [k])

        if k in TRAVEL["d2"]:
            send("d2", k, landing("l2", k), "down", "right")
        finish_three((k[0], k[1] + 1))
    for k in ((1, -1), (0, 0), (-1, -1), (0, -1)):
        finish_three(k)

    corners = [(-1, -1), (-1, 0), (0, -1), (0, 0)]
    for y in range(4):
        update_parent(3, mine[3], corners[3], corners[y])
    start_strip("A3")
    pass_strip("E2")
    for x in range(3):
        for y in range(x + 1):
            update_parent(x, mine[3], corners[x], corners[y])
    pass_strip("A3")

    @pl.when(has["right"])
    def _():
        update_parent(1, from_right, (-1, -1), (-1, -1))

    @pl.when(has["up"])
    def _():
        receive("v2", (1, 0), from_down)
        receive("v2", (1, 1), from_down)
        update_parent(0, from_down, (1, 0), (1, 0))
        update_parent(1, from_down, (1, 1), (1, 0))
        update_parent(1, from_down, (1, 1), (1, 1))
        receive("v3", (1, -1), from_down)
        receive("v3", (1, 0), from_down)
        update_parent(0, from_down, (1, -1), (1, -1))
        update_parent(1, from_down, (1, 0), (1, -1))
        update_parent(1, from_down, (1, 0), (1, 0))

    @pl.when(has["up"] & has["right"])
    def _():
        receive("d2", (1, -1), other)
        update_parent(1, other, (1, -1), (1, -1))

    start_strip("A1")

    @pl.when(has["left"])
    def _():
        for k in TRAVEL["r3"]:
            receive("r3", k, from_left)

    send("d3", (1, 1), landing("r3", (1, 1)), "down", "left")

    @pl.when(has["left"])
    def _():
        update_parent(0, from_left, (-1, 1), (-1, 1))
        update_parent(2, from_left, (0, 1), (-1, 1))
        update_parent(2, from_left, (0, 1), (0, 1))

    pass_strip("A1")

    @pl.when(has["up"] & has["left"])
    def _():
        receive("d3", (1, 1), other)
        update_parent(0, other, (1, 1), (1, 1))

    start_strip("A2")
    pass_strip("A2")
    for name in ("E2", "A3", "A1", "A2"):
        end_strip(name)
    for copy, way, and_also in sent:
        if and_also is None:
            pl.when(has[way])(copy.wait_send)
        else:
            pl.when(has[way] & has[and_also])(copy.wait_send)
    for name in STRIPS:
        strip_copy(name, True).wait_send()
        strip_copy(name, False).wait_send()


def local(near, interp, red_count, owner_flip):
    points, slots = near.shape[-1], interp.shape[-1]
    boxes = near.reshape(4, 9, points, points)
    strip_width = strip_places(slots)[1]
    small_rows = 2 * slots * slots // points
    any_space = pl.BlockSpec(memory_space=pl.ANY)
    parent = pl.pallas_call(
        functools.partial(kernel, (lax.axis_size("row"), lax.axis_size("col"))),
        out_shape=jax.ShapeDtypeStruct((4 * slots, 4 * slots), jnp.float32),
        in_specs=[any_space, any_space] + [pl.BlockSpec(memory_space=pltpu.SMEM)] * 2,
        out_specs=pl.BlockSpec(memory_space=pltpu.VMEM),
        scratch_shapes=[
            pltpu.VMEM((4, 9, points, points), jnp.float32),
            pltpu.VMEM((4, slots, slots), jnp.float32),
            pltpu.VMEM((4, 9, slots, points), jnp.float32),
            pltpu.VMEM((4, slots, 3 * points), jnp.bfloat16),
            pltpu.VMEM((2, 9, 4 * slots, points), jnp.bfloat16),
            pltpu.VMEM((COUNT, slots, points), jnp.float32),
            pltpu.VMEM((len(PACKED), small_rows, points // 2), jnp.float32),
            pltpu.VMEM((len(PACKED), small_rows, points // 2), jnp.float32),
            pltpu.VMEM((4, 9, 4 * slots, points), jnp.bfloat16),
            pltpu.VMEM((12, slots, points), jnp.float32),
            pltpu.VMEM((slots, strip_width), jnp.float32),
            pltpu.VMEM((slots, strip_width), jnp.float32),
            pltpu.VMEM((slots, strip_width), jnp.float32),
            pltpu.VMEM((slots, strip_width), jnp.float32),
            pltpu.SemaphoreType.DMA((COUNT,)),
            pltpu.SemaphoreType.DMA((COUNT,)),
            pltpu.SemaphoreType.DMA((20,)),
            pltpu.SemaphoreType.DMA((2 * len(STRIPS),)),
            pltpu.SemaphoreType.DMA((2 * len(STRIPS),)),
        ],
        compiler_params=pltpu.CompilerParams(
            vmem_limit_bytes=60 * 2**20, collective_id=0, has_side_effects=True
        ),
        name="skeletonize",
    )(boxes, interp, red_count, owner_flip)
    return parent[None, None]


def solution(mesh):
    in_specs = (
        P("row", "col", None, None, None, None),
        P("row", "col", None, None),
        P("row", "col"),
        P("row", "col", None),
    )
    out_specs = P("row", "col", None, None)
    return jax.shard_map(local, mesh=mesh, in_specs=in_specs, out_specs=out_specs, check_vma=False)
```

time: 165 us -> 116 us (0.70)
  the two profiles are of different devices: /device:TPU:22 before, /device:TPU:0 now
where the time goes in v2:
time: 116 us
  Pallas kernels  113 us (97%)
  local copies, waits for them, and re-layouts  2.7 us (2%)
    pallas_call x1, Pallas kernels, local(): pl.pallas_call(functools.partial(kernel, (lax.axis_size('row'), lax.axis_...  113 us
    unnamed x1, local copies, waits for them, and re-layouts  2.7 us

profile of v2, /device:TPU:0, one launch (start us, length us, event | category | flops | bytes accessed | tf_op | source)
XLA Modules:
  0.0 116.0 jit_solution(9406448484540733458)
XLA Ops:
  0.0 113.3 %skeletonize.1 = f32[640,640]{1,0:T(8,128)} custom-call(f32[4,9,256,256]{3,2,1,0:T(8,128)} %bitcast.2, f32[2,2,160,160]{3,2,1,0:T(8,128)} %interp_all.1, s32[2,2]{1,0:T(2,128)} %counts.1, s32[1,1,2]{2,1,0:T(1,128)} %flip.1), custom_call_target="tpu_custom_call" | custom-call | tf_op jit(solution)/shard_map/skeletonize/pallas_call | solution.py:635
  113.3 2.7 %copy.6 = f32[1,1,640,640]{3,2,1,0:T(8,128)} copy(f32[1,1,640,640]{3,2,1,0:T(8,128)} %bitcast.3) | data formatting | bytes 3276800

commit v3 on v2

--- a/solution.py
+++ b/solution.py
@@ -54,6 +54,7 @@
 
 PACKED = {("l0", (0, 0)), ("r1", (0, 1)), ("r1", (0, 0)), ("d0", (0, 0)), ("d1", (0, 1)), ("d1", (0, 0))}
 PACKED |= {(name, k) for name in ("l2", "r3", "d2", "d3") for k in TRAVEL[name]} - {("l2", (0, -1))}
+PACKED |= {("u0", (0, 0)), ("u1", (0, -1)), ("u1", (0, 0)), ("u1", (0, 1))}
 PACKED = sorted(PACKED)
 
 
@@ -382,7 +383,6 @@
         receive("l0", (0, -1), from_right)
         update(1, from_right, (0, -1), [(0, -1)])
 
-    send("d0", (0, -1), landing("l0", (0, -1)), "up", "right")
     make_one = panel_maker(1)
 
     def finish_one(k):
@@ -398,7 +398,7 @@
             receive("l0", k, from_right)
             update(1, from_right, (0, -1), [k])
 
-        if k in TRAVEL["d0"]:
+        if k in TRAVEL["d0"][2:]:
             send("d0", k, landing("l0", k), "up", "right")
         finish_one((k[0], k[1] + 1))
 
@@ -426,6 +426,9 @@
         arrive("r1", (-1, 1))
 
     send("d1", (-1, 1), landing("r1", (-1, 1)), "up", "left")
+    for k in TRAVEL["d0"][:2]:
+        send("d0", k, landing("l0", k), "up", "right")
+    start_strip("E2")
 
     @pl.when(has["down"] & has["left"])
     def _():
@@ -528,7 +531,6 @@
         receive("l2", (0, -1), from_right)
         update(3, from_right, (0, -1), [(0, -1)])
 
-    start_strip("E2")
     make_three = panel_maker(3)
     pass_strip("E3")
     update_parent(0, mine[2], (-1, 0), (-1, 0))

time: 116 us -> 129 us (1.11)
  Pallas kernels: 113 us -> 126 us
    pallas_call x1, Pallas kernels: 113 us -> 126 us  [local(): pl.pallas_call(functools.partial(kernel, (lax.axis_size('row'), lax.axis_...]
where the time goes in v3:
time: 129 us
  Pallas kernels  126 us (98%)
  local copies, waits for them, and re-layouts  2.7 us (2%)
    pallas_call x1, Pallas kernels, local(): pl.pallas_call(functools.partial(kernel, (lax.axis_size('row'), lax.axis_...  126 us
    unnamed x1, local copies, waits for them, and re-layouts  2.7 us

profile of v3, /device:TPU:0, one launch (start us, length us, event | category | flops | bytes accessed | tf_op | source)
XLA Modules:
  0.0 129.0 jit_solution(15507918283562776123)
XLA Ops:
  0.0 126.3 %skeletonize.1 = f32[640,640]{1,0:T(8,128)} custom-call(f32[4,9,256,256]{3,2,1,0:T(8,128)} %bitcast.2, f32[2,2,160,160]{3,2,1,0:T(8,128)} %interp_all.1, s32[2,2]{1,0:T(2,128)} %counts.1, s32[1,1,2]{2,1,0:T(1,128)} %flip.1), custom_call_target="tpu_custom_call" | custom-call | tf_op jit(solution)/shard_map/skeletonize/pallas_call | solution.py:637
  126.3 2.7 %copy.6 = f32[1,1,640,640]{3,2,1,0:T(8,128)} copy(f32[1,1,640,640]{3,2,1,0:T(8,128)} %bitcast.3) | data formatting | bytes 3276800
